TPU v7x, 128 devices: a whole 4x4x4 slice. The times are simulated.
128 devices in a mesh: wave: 8 (over y, z_lo), pix: 16 (over x, z_hi, core).
Axes of the slice: x: 4, y: 4, z: 4 (z_hi: 2, z_lo: 2; z = z_hi * 2 + z_lo), core: 2. Of those that a mesh axis runs over, the one named last changes fastest.
Arguments:
- raw_spectra: bfloat16 [2, 2, 16384, 2048], P(None, None, 'wave', 'pix'), may hold values from -6 to 6
- background: float32 [16384], P('wave'), may hold values from -6 to 6
- dispersion: float32 [16384], P('wave'), may hold values from -3.140625 to 3.140625
- propagator: bfloat16 [2, 2048, 2048], P(None, None, 'pix'), may hold values from -0.09375 to 0.09375
Outputs:
- image: float32 [2, 2, 16384, 2048], P(None, None, ('wave', 'pix'))
All inputs are finite; a program needn't handle non-finite values.
Results may differ from a plain program's by a relative error of at most 0.0029.
Values may be sent and summed in bfloat16 or wider, within the bound.
A program may use at most 128 MiB of HBM per device.

v0:
```python
import math

import jax
import jax.numpy as jnp
from jax import lax
from jax.sharding import PartitionSpec as P

BLOCK = 1024


HIGHEST_PRECISION = lax.Precision.HIGHEST


def from_partner(value, axis, apart):
    mask = 2**apart
    pairs = [(source, source ^ mask) for source in range(lax.axis_size(axis))]
    return lax.ppermute(value, axis, pairs)


def twiddle_table(left_index, right_index, modulus):
    product = left_index[:, None] * right_index[None, :] % modulus
    phase_angle = -2.0 * math.pi / modulus * product.astype(jnp.float32)
    return (jnp.cos(phase_angle), jnp.sin(phase_angle))


def rotate(values, cosine, sine_part):
    return jnp.stack(
        (values[0] * cosine - values[1] * sine_part, values[0] * sine_part + values[1] * cosine)
    )


def local_transform(spectrum, block_size):
    length = spectrum.shape[2]
    radix_size = length // block_size
    shaped = spectrum.reshape(spectrum.shape[:2] + (radix_size, block_size) + spectrum.shape[3:])
    small_cos, small_sin = twiddle_table(
        jnp.arange(radix_size, dtype=jnp.int32), jnp.arange(radix_size, dtype=jnp.int32), radix_size
    )
    real_sum = jnp.einsum(
        "xrbp,ru->xubp", shaped[0], small_cos, precision=HIGHEST_PRECISION
    ) - jnp.einsum("xrbp,ru->xubp", shaped[1], small_sin, precision=HIGHEST_PRECISION)
    imag_sum = jnp.einsum(
        "xrbp,ru->xubp", shaped[0], small_sin, precision=HIGHEST_PRECISION
    ) + jnp.einsum("xrbp,ru->xubp", shaped[1], small_cos, precision=HIGHEST_PRECISION)
    turn_cos, turn_sin = twiddle_table(
        jnp.arange(radix_size, dtype=jnp.int32), jnp.arange(block_size, dtype=jnp.int32), length
    )
    mixed_terms = rotate(
        jnp.stack((real_sum, imag_sum)), turn_cos[:, :, None], turn_sin[:, :, None]
    )
    big_cos, big_sin = twiddle_table(
        jnp.arange(block_size, dtype=jnp.int32), jnp.arange(block_size, dtype=jnp.int32), block_size
    )
    out_real = jnp.einsum(
        "xubp,bv->xuvp", mixed_terms[0], big_cos, precision=HIGHEST_PRECISION
    ) - jnp.einsum("xubp,bv->xuvp", mixed_terms[1], big_sin, precision=HIGHEST_PRECISION)
    out_imag = jnp.einsum(
        "xubp,bv->xuvp", mixed_terms[0], big_sin, precision=HIGHEST_PRECISION
    ) + jnp.einsum("xubp,bv->xuvp", mixed_terms[1], big_cos, precision=HIGHEST_PRECISION)
    return jnp.stack((out_real, out_imag))


def on_device(raw_spectra, background, dispersion, propagator):
    row_count = raw_spectra.shape[1]
    wave_span = raw_spectra.shape[2]
    pix_local = raw_spectra.shape[3]
    wave_count = lax.axis_size("wave")
    pix_count = lax.axis_size("pix")
    devices = wave_count * pix_count
    length = wave_span * wave_count
    wave_pos = lax.axis_index("wave")
    bit_count = wave_count.bit_length() - 1
    real_part = raw_spectra[0].astype(jnp.float32) - background[None, :, None]
    imag_part = raw_spectra[1].astype(jnp.float32)
    spectrum = rotate(
        jnp.stack((real_part, imag_part)),
        jnp.cos(dispersion)[None, :, None],
        jnp.sin(dispersion)[None, :, None],
    )
    for section_index in range(bit_count):
        bit_index = bit_count - 1 - section_index
        half_span = 1 << bit_index
        partner = from_partner(spectrum, "wave", bit_index)
        upper_half = wave_pos // half_span % 2 == 1
        phase_angle = -math.pi / half_span * (wave_pos % half_span).astype(jnp.float32)
        turned = rotate(partner - spectrum, jnp.cos(phase_angle), jnp.sin(phase_angle))
        spectrum = jnp.where(upper_half, turned, spectrum + partner)
    owner_index = jnp.int32(0)
    for bit_index in range(bit_count):
        owner_index = owner_index + wave_pos // (1 << bit_index) % 2 * (
            1 << bit_count - 1 - bit_index
        )
    positions = jnp.arange(wave_span, dtype=jnp.int32)
    phase_angle = -2.0 * math.pi / length * (positions * owner_index % length).astype(jnp.float32)
    spectrum = rotate(
        spectrum, jnp.cos(phase_angle)[None, :, None], jnp.sin(phase_angle)[None, :, None]
    )
    transform = local_transform(spectrum, BLOCK)
    radix_size = transform.shape[2]
    depth_bf = (transform * (1.0 / math.sqrt(length))).astype(jnp.bfloat16)
    depth_width = BLOCK // devices
    outgoing = depth_bf.reshape(
        2, row_count, radix_size, wave_count, pix_count, depth_width, pix_local
    )
    merged = outgoing.reshape(2, row_count, radix_size, devices, depth_width, pix_local)
    arrived = lax.all_to_all(
        merged, ("wave", "pix"), split_axis=3, concat_axis=3, tiled=True
    ).reshape(outgoing.shape)
    bit_shape = (2,) * bit_count
    dim_count = len(bit_shape)
    spread = arrived.reshape(
        (2, row_count, radix_size) + bit_shape + (pix_count, depth_width, pix_local)
    )
    wave_axes = tuple(range(3, 3 + dim_count))
    wave_axes = wave_axes[::-1]
    axis_order = (0, 1, 4 + dim_count, 2) + wave_axes + (3 + dim_count, 5 + dim_count)
    depth_field = jnp.transpose(spread, axis_order).reshape(
        2, row_count, depth_width * radix_size * wave_count, pix_count * pix_local
    )
    column_piece = lax.all_gather(propagator, "pix", axis=2, tiled=True)
    image_real = jnp.dot(
        depth_field[0], column_piece[0], preferred_element_type=jnp.float32
    ) - jnp.dot(depth_field[1], column_piece[1], preferred_element_type=jnp.float32)
    image_imag = jnp.dot(
        depth_field[0], column_piece[1], preferred_element_type=jnp.float32
    ) + jnp.dot(depth_field[1], column_piece[0], preferred_element_type=jnp.float32)
    return jnp.stack((image_real, image_imag))


def solution(mesh):
    in_specs = (P(None, None, "wave", "pix"), P("wave"), P("wave"), P(None, None, "pix"))
    out_specs = P(None, None, ("wave", "pix"), None)
    return jax.shard_map(
        on_device, mesh=mesh, in_specs=in_specs, out_specs=out_specs, check_vma=False
    )
```

profile of v0, /device:TPU:1, one launch (start us, length us, event | category | flops | bytes accessed | tf_op | source)
XLA Modules:
  0.0 539.1 jit_solution(3997361140519141677)
XLA Ops:
  8.0 3.6 fusion.23
  14.3 3.7 collective-permute-start
  18.3 90.1 %collective-permute-done = f32[2,2,2048,128]{3,2,1,0:T(8,128)} collective-permute-done((f32[2,2,2048,128]{3,2,1,0:T(8,128)}, f32[2,2,2048,128]{3,2,1,0:T(8,128)}, u32[]{:S(2)}, u32[]{:S(2)}) %collective-permute-start) | collective-permute-done | bytes 4194336 | tf_op jit(solution)/shard_map/ppermute | solution.py:17
  108.4 3.4 fusion.100
  113.8 5.3 maximum_select_fusion
  120.6 89.4 %collective-permute-done.1 = f32[2,2,2048,128]{3,2,1,0:T(8,128)} collective-permute-done((f32[2,2,2048,128]{3,2,1,0:T(8,128)}, f32[2,2,2048,128]{3,2,1,0:T(8,128)}, u32[]{:S(2)}, u32[]{:S(2)}) %collective-permute-start.1) | collective-permute-done | bytes 4194336 | tf_op jit(solution)/shard_map/ppermute | solution.py:17
  210.0 5.6 %fusion.112 = f32[2,2,2048,128]{3,2,1,0:T(8,128)S(1)} fusion(f32[2,2,2048,128]{3,2,1,0:T(8,128)} %collective-permute-done.1, f32[2,2,2048,128]{3,2,1,0:T(8,128)} %collective-permute-done, f32[1,2,2048,128]{3,2,1,0:T(8,128)} %copy-done, f32[1,2,2048,128]{3,2,1,0:T(8,128)S(1)} %get-tuple-element.15, f32[1,2,2048,128]{3,2,1,0:T(8,128)} %copy-done.5, ...), kind=kLoop, calls=%fused_computation.127 | loop fusion | flops 5242880 | bytes 20971520 | tf_op jit(solution)/shard_map/sub | solution.py:86
  218.4 5.6 %maximum_select_fusion.1 = f32[2,2,2048,128]{3,2,1,0:T(8,128)} fusion(f32[1,2,2048,128]{3,2,1,0:T(8,128)S(1)} %get-tuple-element.12, f32[1,2,2048,128]{3,2,1,0:T(8,128)S(1)} %get-tuple-element.11, f32[2,2,2048,128]{3,2,1,0:T(8,128)} %collective-permute-done.1, pred[]{:T(512)S(6)} %eq.28, f32[2,2,2048,128]{3,2,1,0:T(8,128)} %collective-permute-done, ...), kind=kLoop, calls=%fused_computation.14 | loop fusion | flops 7340032 | bytes 25165826 | tf_op jit(solution)/shard_map/jit(_where)/select_n | solution.py:87
  228.7 85.7 %collective-permute-done.2 = f32[2,2,2048,128]{3,2,1,0:T(8,128)} collective-permute-done((f32[2,2,2048,128]{3,2,1,0:T(8,128)}, f32[2,2,2048,128]{3,2,1,0:T(8,128)}, u32[]{:S(2)}, u32[]{:S(2)}) %collective-permute-start.2) | collective-permute-done | bytes 4194336 | tf_op jit(solution)/shard_map/ppermute | solution.py:17
  314.4 3.9 sub.78
  318.6 4.2 maximum_select_fusion.2
  323.1 9.2 %multiply_subtract_fusion = f32[2,2,1024,128]{3,1,2,0:T(2,128)S(1)} fusion(f32[2,2,1024,128]{3,2,1,0:T(8,128)S(1)} %bitcast.87, f32[2,2,1024,128]{3,2,1,0:T(8,128)S(1)} %bitcast.84, f32[2,1024]{0,1:T(8,128)S(1)} %copy.27, f32[2,1024]{0,1:T(8,128)S(1)} %copy.25), kind=kLoop, calls=%fused_computation.45 | loop fusion | flops 1572864 | bytes 6307840 | tf_op jit(solution)/shard_map/sub | solution.py:28
  332.4 7.9 %fusion.57 = f32[2,2,1024,128]{3,0,2,1:T(2,128)S(1)} fusion(f32[2,2,1024,128]{3,1,2,0:T(2,128)S(1)} %multiply_subtract_fusion), kind=kOutput, calls=%fused_computation.84 | convolution fusion | flops 12582968 | bytes 4194304 | tf_op jit(solution)/shard_map/xrbp,ru->xubp/dot_general | solution.py:39
  340.3 7.9 %fusion.59 = f32[2,2,1024,128]{3,0,2,1:T(2,128)S(1)} fusion(f32[2,2,1024,128]{3,1,2,0:T(2,128)S(1)} %multiply_subtract_fusion), kind=kOutput, calls=%fused_computation.86 | convolution fusion | flops 12582968 | bytes 4194304 | tf_op jit(solution)/shard_map/xrbp,ru->xubp/dot_general | solution.py:42
  348.3 12.1 %convolution_subtract_fusion = f32[2,2,1024,128]{3,0,2,1:T(2,128)S(1)} fusion(f32[2,2,1024,128]{3,0,2,1:T(2,128)S(1)} %fusion.57, f32[2,2,1024,128]{3,2,1,0:T(8,128)S(1)} %bitcast.88, f32[2,2,1024,128]{3,2,1,0:T(8,128)S(1)} %bitcast.85, f32[2,1024]{0,1:T(8,128)S(1)} %copy.27, f32[2,1024]{0,1:T(8,128)S(1)} %copy.25), kind=kOutput, calls=%fused_computation.60 | convolution fusion | flops 14680120 | bytes 8404992 | tf_op jit(solution)/shard_map/xrbp,ru->xubp/dot_general | solution.py:41
  360.4 15.4 %subtract_bitcast_fusion.1 = (f32[2,2,1024,128]{3,1,2,0:T(2,128)S(1)}, f32[2,2,1024,128]{3,1,2,0:T(2,128)S(1)}) fusion(f32[2,2,1024,128]{3,0,2,1:T(2,128)S(1)} %convolution_subtract_fusion, f32[2,1024]{0,1:T(8,128)S(1)} %copy-done.9, f32[2,1024]{0,1:T(8,128)S(1)} %copy-done.8, f32[2,2,1024,128]{3,0,2,1:T(2,128)S(1)} %fusion.59, ...), kind=kOutput, calls=%fused_computation.43 | convolution fusion | flops 17825848 | bytes 12615680 | tf_op jit(solution)/shard_map/xrbp,ru->xubp/dot_general | solution.py:44
  375.8 22.1 %fusion.10 = f32[1024,2,2,128]{3,0,2,1:T(8,128)S(1)} fusion(f32[2,2,1024,128]{3,1,2,0:T(2,128)S(1)} %get-tuple-element.5), kind=kOutput, calls=%fused_computation.22 | convolution fusion | flops 6457131008 | bytes 4194304 | tf_op jit(solution)/shard_map/xubp,bv->xuvp/dot_general | solution.py:54
  397.9 22.5 %fusion.8 = f32[1024,2,2,128]{3,0,2,1:T(8,128)S(1)} fusion(f32[2,2,1024,128]{3,1,2,0:T(2,128)S(1)} %get-tuple-element.6), kind=kOutput, calls=%fused_computation.20 | convolution fusion | flops 6457131008 | bytes 4194304 | tf_op jit(solution)/shard_map/xubp,bv->xuvp/dot_general | solution.py:59
  420.4 22.8 %subtract_bitcast_fusion = f32[1,2,2,128,8,128]{5,4,3,2,1,0:T(8,128)S(1)} fusion(f32[1024,2,2,128]{3,0,2,1:T(8,128)S(1)} %fusion.10, f32[2,2,1024,128]{3,1,2,0:T(2,128)S(1)} %get-tuple-element.6), kind=kOutput, calls=%fused_computation.41 | convolution fusion | flops 6457655296 | bytes 6291456 | tf_op jit(solution)/shard_map/xubp,bv->xuvp/dot_general | solution.py:56
  443.2 22.6 %add_bitcast_fusion = f32[1,2,2,128,8,128]{5,4,3,2,1,0:T(8,128)S(1)} fusion(f32[1024,2,2,128]{3,0,2,1:T(8,128)S(1)} %fusion.8, f32[2,2,1024,128]{3,1,2,0:T(2,128)S(1)} %get-tuple-element.5), kind=kOutput, calls=%fused_computation.40 | convolution fusion | flops 6457655296 | bytes 6291456 | tf_op jit(solution)/shard_map/xubp,bv->xuvp/dot_general | solution.py:57
  466.4 42.2 %all_to_all.5 = bf16[2,2,2,128,8,128]{5,4,2,1,0,3:T(8,128)(2,1)S(1)} all-to-all(bf16[2,2,2,128,8,128]{5,4,2,1,0,3:T(8,128)(2,1)S(1)} %fusion.7), channel_id=1, replica_groups=mesh['wave'=8,'pix'=16] {'wave','pix'}, dimensions={3} | all-to-all | bytes 4194304 | tf_op jit(solution)/shard_map/all_to_all | solution.py:106
  511.5 6.1 %fusion.1 = f32[2,128,2048]{2,1,0:T(8,128)S(1)} fusion(bf16[2,128,2048]{2,1,0:T(8,128)(2,1)S(1)} %squeeze.14, bf16[2,2048,2048]{2,1,0:T(8,128)(2,1)} %all-gather.2.cloned.1.call-done), kind=kOutput, calls=%fused_computation.3 | convolution fusion | flops 2147483648 | bytes 11534336 | tf_op jit(solution)/shard_map/dot_general | solution.py:121
  517.7 5.9 %fusion = f32[2,128,2048]{2,1,0:T(8,128)S(1)} fusion(bf16[2,128,2048]{2,1,0:T(8,128)(2,1)S(1)} %squeeze.16, bf16[2,2048,2048]{2,1,0:T(8,128)(2,1)} %all-gather.2.cloned.1.call-done), kind=kOutput, calls=%fused_computation.2 | convolution fusion | flops 2147483648 | bytes 11534336 | tf_op jit(solution)/shard_map/dot_general | solution.py:126
  523.6 3.6 fusion.20
  (54 shorter events, 23.7 us)
Async XLA Ops:
  6.5 505.0 %all-gather.2.cloned.1.call-start = ((), (), s32[]{:S(2)}) async-start(), calls=%async_computation.1 | async-start | bytes 17825792 | tf_op jit(solution)/shard_map/all_gather | solution.py:120
  11.6 2.7 copy-start
  14.3 94.1 %collective-permute-start = (f32[2,2,2048,128]{3,2,1,0:T(8,128)}, f32[2,2,2048,128]{3,2,1,0:T(8,128)}, u32[]{:S(2)}, u32[]{:S(2)}) collective-permute-start(f32[2,2,2048,128]{3,2,1,0:T(8,128)} %pad_maximum_fusion), channel_id=1, source_target_pairs={{0,64},{16,80},{32,96},{48,112},{64,0},{80,16},{96,32},{112,48},{1... | collective-permute-start | bytes 12582920 | tf_op jit(solution)/shard_map/ppermute | solution.py:17
  111.8 2.0 copy-start.1
  112.2 6.9 %copy-start.3 = (f32[1,2,2048,128]{3,2,1,0:T(8,128)}, f32[1,2,2048,128]{3,2,1,0:T(8,128)S(1)}, u32[]{:S(2)}) copy-start(f32[1,2,2048,128]{3,2,1,0:T(8,128)S(1)} %get-tuple-element.13) | copy-start | bytes 6291460
  112.3 6.9 %copy-start.5 = (f32[1,2,2048,128]{3,2,1,0:T(8,128)}, f32[1,2,2048,128]{3,2,1,0:T(8,128)S(1)}, u32[]{:S(2)}) copy-start(f32[1,2,2048,128]{3,2,1,0:T(8,128)S(1)} %get-tuple-element.14) | copy-start | bytes 6291460
  119.1 90.9 %collective-permute-start.1 = (f32[2,2,2048,128]{3,2,1,0:T(8,128)}, f32[2,2,2048,128]{3,2,1,0:T(8,128)}, u32[]{:S(2)}, u32[]{:S(2)}) collective-permute-start(f32[2,2,2048,128]{3,2,1,0:T(8,128)} %maximum_select_fusion), channel_id=1, source_target_pairs={{0,32},{16,48},{32,0},{48,16},{64,96},{80,112},{96,64},{112,80},{1... | collective-permute-start | bytes 12582920 | tf_op jit(solution)/shard_map/ppermute | solution.py:17
  215.6 1.6 copy-start.2
  215.6 2.2 copy-start.4
  215.6 2.8 copy-start.6
  224.0 90.4 %collective-permute-start.2 = (f32[2,2,2048,128]{3,2,1,0:T(8,128)}, f32[2,2,2048,128]{3,2,1,0:T(8,128)}, u32[]{:S(2)}, u32[]{:S(2)}) collective-permute-start(f32[2,2,2048,128]{3,2,1,0:T(8,128)} %maximum_select_fusion.1), channel_id=1, source_target_pairs={{0,16},{16,0},{32,48},{48,32},{64,80},{80,64},{96,112},{112,96},{1... | collective-permute-start | bytes 12582920 | tf_op jit(solution)/shard_map/ppermute | solution.py:17
  348.3 12.1 %copy-start.8 = (f32[2,1024]{0,1:T(8,128)S(1)}, f32[2,1024]{0,1:T(8,128)}, u32[]{:S(2)}) copy-start(f32[2,1024]{0,1:T(8,128)} %copy.31) | copy-start | bytes 24580
  348.3 12.1 %copy-start.9 = (f32[2,1024]{0,1:T(8,128)S(1)}, f32[2,1024]{0,1:T(8,128)}, u32[]{:S(2)}) copy-start(f32[2,1024]{0,1:T(8,128)} %copy.32) | copy-start | bytes 24580
  511.5 6.2 %copy-start.7 = (bf16[2,128,2048]{2,1,0:T(8,128)(2,1)}, bf16[2,128,2048]{2,1,0:T(8,128)(2,1)S(1)}, u32[]{:S(2)}) copy-start(bf16[2,128,2048]{2,1,0:T(8,128)(2,1)S(1)} %squeeze.16) | copy-start | bytes 3145732
  511.5 12.0 %slice-start = ((s8[16777216]{0:T(1024)(128)(4,1)}), s8[4194304]{0:T(1024)(128)(4,1)S(1)}, s32[]{:S(2)}) async-start(s8[16777216]{0:T(1024)(128)(4,1)} %bitcast.92), calls=%async_computation.2 | async-start | bytes 8388608
  511.5 12.0 %slice-start.1 = ((s8[16777216]{0:T(1024)(128)(4,1)}), s8[4194304]{0:T(1024)(128)(4,1)S(1)}, s32[]{:S(2)}) async-start(s8[16777216]{0:T(1024)(128)(4,1)} %bitcast.92), calls=%async_computation.3 | async-start | bytes 8388608
  517.6 5.9 %slice-start.2 = ((s8[16777216]{0:T(1024)(128)(4,1)}), s8[4194304]{0:T(1024)(128)(4,1)S(1)}, s32[]{:S(2)}) async-start(s8[16777216]{0:T(1024)(128)(4,1)} %bitcast.92), calls=%async_computation.4 | async-start | bytes 8388608
  517.7 5.9 %slice-start.3 = ((s8[16777216]{0:T(1024)(128)(4,1)}), s8[4194304]{0:T(1024)(128)(4,1)S(1)}, s32[]{:S(2)}) async-start(s8[16777216]{0:T(1024)(128)(4,1)} %bitcast.92), calls=%async_computation.5 | async-start | bytes 8388608
Sparse Core Ops, SparseCore 0:
  9.6 126.9 all-gather.1
where the time goes:
time: 545 us; the launch traced here: 539 us
  waiting for transfers between devices  266 us (49%)
  matrix products  151 us (28%)
  other arithmetic  47.9 us (9%)
  blocking collectives  42.2 us (8%)
  between operations  14.4 us (3%)
  local copies, waits for them, and re-layouts  10.6 us (2%)
  starting transfers between devices  6.73 us (1%)
    ppermute x3, waiting for transfers between devices, from_partner(): return lax.ppermute(value, axis, pairs)  265 us
    all_to_all x1, blocking collectives, on_device(): lax.all_to_all(merged, ('wave', 'pix'), split_axis=3, concat_axis=3, tile...  42.2 us
    dot_general x1, matrix products, local_transform(): jnp.einsum('xubp,bv->xuvp', mixed_terms[1], big_sin, precision=HIGHEST_PR...  22.8 us
    dot_general x1, matrix products, local_transform(): jnp.einsum('xubp,bv->xuvp', mixed_terms[0], big_sin, precision=HIGHEST_PR...  22.6 us
    dot_general x1, matrix products, local_transform(): jnp.einsum('xubp,bv->xuvp', mixed_terms[1], big_cos, precision=HIGHEST_PR...  22.5 us
    dot_general x1, matrix products, local_transform(): jnp.einsum('xubp,bv->xuvp', mixed_terms[0], big_cos, precision=HIGHEST_PR...  22.1 us
    dot_general x1, matrix products, local_transform(): jnp.einsum('xrbp,ru->xubp', shaped[1], small_cos, precision=HIGHEST_PRECI...  15.4 us
    select_n x3, other arithmetic, on_device(): spectrum = jnp.where(upper_half, turned, spectrum + partner)  15.2 us
  transfers between devices with their start and end apart: 4, of which 3 were waited for; matrix products, arithmetic and copies ran while one was open for 34% of the time, Pallas kernels for 0%

commit v1 on v0

v1 whole, which is shorter than its diff:
```python
import math

import jax
import jax.numpy as jnp
from jax import lax
from jax.sharding import PartitionSpec as P

HIGHEST_PRECISION = lax.Precision.HIGHEST


def twiddle_table(left_index, right_index, modulus, scale=1.0):
    product = left_index[:, None] * right_index[None, :] % modulus
    phase_angle = -2.0 * math.pi / modulus * product.astype(jnp.float32)
    return (jnp.cos(phase_angle) * scale, jnp.sin(phase_angle) * scale)


def complex_contract(spec, real, imag, cosine, sine_part):
    def dot(a, b):
        return jnp.einsum(spec, a, b, precision=HIGHEST_PRECISION)

    return (dot(real, cosine) - dot(imag, sine_part), dot(real, sine_part) + dot(imag, cosine))


def on_device(raw_spectra, background, dispersion, propagator):
    row_count = raw_spectra.shape[1]
    wave_span = raw_spectra.shape[2]
    pix_local = raw_spectra.shape[3]
    wave_count = lax.axis_size("wave")
    pix_count = lax.axis_size("pix")
    devices = wave_count * pix_count
    length = wave_span * wave_count
    sub_pix = pix_local // wave_count
    first = length // devices
    second = devices

    pieces = raw_spectra.reshape(2, row_count, wave_span, wave_count, sub_pix)
    pieces = jnp.transpose(pieces, (3, 0, 1, 4, 2))
    pieces = lax.all_to_all(pieces, "wave", 0, 0, tiled=True)
    full_background = lax.all_gather(background, "wave", tiled=True)
    full_dispersion = lax.all_gather(dispersion, "wave", tiled=True)

    spectra = jnp.transpose(pieces, (1, 2, 3, 0, 4)).reshape(2, row_count, sub_pix, length)
    real_part = spectra[0].astype(jnp.float32) - full_background
    imag_part = spectra[1].astype(jnp.float32)
    cosine = jnp.cos(full_dispersion)
    sine_part = jnp.sin(full_dispersion)
    turned_real = real_part * cosine - imag_part * sine_part
    turned_imag = real_part * sine_part + imag_part * cosine

    shape = (row_count, sub_pix, first, second)
    turned_real = turned_real.reshape(shape)
    turned_imag = turned_imag.reshape(shape)
    index_first = jnp.arange(first, dtype=jnp.int32)
    index_second = jnp.arange(second, dtype=jnp.int32)
    small_cos, small_sin = twiddle_table(index_first, index_first, first)
    stage_real, stage_imag = complex_contract(
        "rsak,az->rszk", turned_real, turned_imag, small_cos, small_sin
    )
    turn_cos, turn_sin = twiddle_table(index_first, index_second, length)
    mixed_real = stage_real * turn_cos - stage_imag * turn_sin
    mixed_imag = stage_real * turn_sin + stage_imag * turn_cos
    big_cos, big_sin = twiddle_table(
        index_second, index_second, second, 1.0 / math.sqrt(length)
    )
    out_real, out_imag = complex_contract(
        "rszk,kt->trsz", mixed_real, mixed_imag, big_cos, big_sin
    )
    depth_bf = jnp.stack((out_real, out_imag), axis=1).astype(jnp.bfloat16)
    arrived = lax.all_to_all(depth_bf, ("wave", "pix"), 0, 0, tiled=True)
    arrived = arrived.reshape(wave_count, pix_count, 2, row_count, sub_pix, first)
    depth_field = jnp.transpose(arrived, (2, 3, 5, 1, 0, 4)).reshape(
        2, row_count, first, pix_count * pix_local
    )
    column_piece = lax.all_gather(propagator, "pix", axis=2, tiled=True)
    image_real = jnp.dot(
        depth_field[0], column_piece[0], preferred_element_type=jnp.float32
    ) - jnp.dot(depth_field[1], column_piece[1], preferred_element_type=jnp.float32)
    image_imag = jnp.dot(
        depth_field[0], column_piece[1], preferred_element_type=jnp.float32
    ) + jnp.dot(depth_field[1], column_piece[0], preferred_element_type=jnp.float32)
    return jnp.stack((image_real, image_imag))


def solution(mesh):
    in_specs = (P(None, None, "wave", "pix"), P("wave"), P("wave"), P(None, None, "pix"))
    out_specs = P(None, None, ("wave", "pix"), None)
    return jax.shard_map(
        on_device, mesh=mesh, in_specs=in_specs, out_specs=out_specs, check_vma=False
    )
```

time: 545 us -> 203 us (0.37)
  waiting for transfers between devices: 266 us -> 0.73 us
  matrix products: 151 us -> 37.6 us
  blocking collectives: 42.2 us -> 121 us
  other arithmetic: 47.9 us -> 4.66 us
  local copies, waits for them, and re-layouts: 10.6 us -> 18.4 us
    ppermute x3 -> x0, waiting for transfers between devices: 265 us -> none  [from_partner(): return lax.ppermute(value, axis, pairs)]
    dot_general x8, matrix products: 133 us -> 20.5 us  [dot(): return jnp.einsum(spec, a, b, precision=HIGHEST_PRECISION)]
    all_gather x0 -> x2, blocking collectives: none -> 68.7 us  [the longest x1 45.8 us: on_device(): full_dispersion = lax.all_gather(dispersion, 'wave', tiled=True)]
    sub x8 -> x0, other arithmetic: 26.8 us -> none  [the longest x5 14 us: rotate(): values[0] * cosine - values[1] * sine_part]
    select_n x3 -> x0, other arithmetic: 15.2 us -> none  [on_device(): spectrum = jnp.where(upper_half, turned, spectrum + partner)]
    convert_element_type x0 -> x4, local copies, waits for them, and re-layouts: none -> 11.1 us  [the longest x2 6.84 us: on_device(): imag_part = spectra[1].astype(jnp.float32)]
    all_to_all x1, blocking collectives: 42.2 us -> 52 us  [on_device(): arrived = lax.all_to_all(depth_bf, ('wave', 'pix'), 0, 0, tiled=True)]
    ppermute x3 -> x0, starting transfers between devices: 6.73 us -> none  [from_partner(): return lax.ppermute(value, axis, pairs)]
  transfers between devices with their start and end apart: 4 -> 2, of which waited for: 3 -> 0; matrix products, arithmetic and copies ran while one was open for 34% -> 20% of each run, Pallas kernels for 0% -> 0%
where the time goes in v1:
time: 203 us; the launch traced here: 202 us
  blocking collectives  121 us (60%)
  matrix products  37.6 us (19%)
  local copies, waits for them, and re-layouts  18.4 us (9%)
  between operations  13.6 us (7%)
  starting transfers between devices  6.51 us (3%)
  other arithmetic  4.66 us (2%)
    all_to_all x1, blocking collectives, on_device(): arrived = lax.all_to_all(depth_bf, ('wave', 'pix'), 0, 0, tiled=True)  52 us
    all_gather x1, blocking collectives, on_device(): full_dispersion = lax.all_gather(dispersion, 'wave', tiled=True)  45.8 us
    all_gather x1, blocking collectives, on_device(): full_background = lax.all_gather(background, 'wave', tiled=True)  23 us
    dot_general x8, matrix products, dot(): return jnp.einsum(spec, a, b, precision=HIGHEST_PRECISION)  20.5 us
    convert_element_type x2, local copies, waits for them, and re-layouts, on_device(): imag_part = spectra[1].astype(jnp.float32)  6.84 us
    all_to_all x1, starting transfers between devices, on_device(): pieces = lax.all_to_all(pieces, 'wave', 0, 0, tiled=True)  6.51 us
    dot_general x1, matrix products, on_device(): jnp.dot(depth_field[1], column_piece[0], preferred_element_type=jnp.float32)  6.48 us
    dot_general x1, matrix products, on_device(): jnp.dot(depth_field[0], column_piece[0], preferred_element_type=jnp.float32)  5.87 us
  transfers between devices with their start and end apart: 2, of which 0 were waited for; matrix products, arithmetic and copies ran while one was open for 20% of the time, Pallas kernels for 0%

profile of v1, /device:TPU:1, one launch (start us, length us, event | category | flops | bytes accessed | tf_op | source)
XLA Modules:
  0.0 202.3 jit_solution(12084375041132204475)
XLA Ops:
  7.3 2.9 %copy.40 = bf16[2,2,2048,128]{2,3,1,0:T(8,128)(2,1)S(1)} copy(bf16[2,2,2048,128]{3,2,1,0:T(8,128)(2,1)} %param.4) | data formatting | bytes 4194304 | tf_op args[0]
  10.2 1.5 copy.41
  11.7 6.5 %all-to-all-start = ((bf16[8,2,2,16,2048]{4,3,2,1,0:T(8,128)(2,1)}), bf16[8,2,2,16,2048]{4,3,2,1,0:T(8,128)(2,1)S(1)}, u32[]{:S(2)}, u32[]{:S(2)}) async-start(bf16[8,2,2,16,2048]{4,3,2,1,0:T(8,128)(2,1)} %copy.41), calls=%async_computation | async-start | bytes 4194304 | tf_op jit(solution)/shard_map/all_to_all | solution.py:38
  18.9 45.8 %all_gather.10 = f32[16384]{0:T(1024)S(1)} all-gather(f32[2048]{0:T(1024)S(1)} %copy-done.2), channel_id=1, replica_groups=mesh['wave'=8,'pix'=16] {'wave'}, dimensions={0}, use_global_device_ids=true | all-gather | bytes 73728 | tf_op jit(solution)/shard_map/all_gather | solution.py:40
  64.7 23.0 %all_gather.9 = f32[16384]{0:T(1024)S(1)} all-gather(f32[2048]{0:T(1024)S(1)} %copy-done.3), channel_id=1, replica_groups=mesh['wave'=8,'pix'=16] {'wave'}, dimensions={0}, use_global_device_ids=true | all-gather | bytes 73728 | tf_op jit(solution)/shard_map/all_gather | solution.py:39
  87.9 1.7 slice_convert_fusion.1
  89.5 2.5 %copy.42 = f32[1,2,16,8,2048]{4,3,2,1,0:T(8,128)} copy(f32[1,2,16,8,2048]{4,2,1,0,3:T(8,128)S(1)} %get-tuple-element.7) | data formatting | bytes 4194304 | tf_op jit(solution)/shard_map/convert_element_type | solution.py:43
  92.1 1.7 reshape.76
  93.8 4.1 %copy.43 = f32[1,2,16,8,2048]{4,3,2,1,0:T(8,128)} copy(f32[1,2,16,8,2048]{4,2,1,0,3:T(8,128)} %get-tuple-element.8) | data formatting | bytes 4194304 | tf_op jit(solution)/shard_map/convert_element_type | solution.py:44
  97.9 2.7 %reshape.77 = f32[2,16,128,128]{3,2,1,0:T(8,128)} reshape(f32[1,2,16,8,2048]{4,3,2,1,0:T(8,128)} %copy.43) | data formatting | bytes 4194304 | tf_op jit(solution)/shard_map/convert_element_type | solution.py:44
  100.6 4.1 %fusion.27 = f32[128,2,16,128]{3,0,2,1:T(8,128)S(1)} fusion(f32[2,16,128,128]{3,2,1,0:T(8,128)} %reshape.77, f32[2,16,128,128]{3,2,1,0:T(8,128)S(1)} %reshape.76, f32[128,128]{1,0:T(8,128)S(1)} %get-tuple-element.10, f32[128,128]{1,0:T(8,128)S(1)} %get-tuple-element.9, f32[128,128]{1,0:T(8,128)S(1)} %bitcast.101), kind=kOutput, calls=%fused_computation.33 | convolution fusion | flops 807632896 | bytes 6488064 | tf_op jit(solution)/shard_map/rsak,az->rszk/dot_general | solution.py:19
  104.7 2.3 %fusion.26 = f32[128,2,16,128]{3,0,2,1:T(8,128)S(1)} fusion(f32[2,16,128,128]{3,2,1,0:T(8,128)S(1)} %copy-done, f32[2,16,128,128]{3,2,1,0:T(8,128)S(1)} %reshape.76, f32[128,128]{1,0:T(8,128)S(1)} %get-tuple-element.10, f32[128,128]{1,0:T(8,128)S(1)} %get-tuple-element.9, f32[128,128]{1,0:T(8,128)S(1)} %bitcast.102), kind=kOutput, calls=%fused_computation.32 | convolution fusion | flops 807632896 | bytes 6488064 | tf_op jit(solution)/shard_map/rsak,az->rszk/dot_general | solution.py:19
  107.0 2.3 %convolution_subtract_fusion = f32[128,2,16,128]{3,0,2,1:T(8,128)S(1)} fusion(f32[128,2,16,128]{3,0,2,1:T(8,128)S(1)} %fusion.27, f32[2,16,128,128]{3,2,1,0:T(8,128)S(1)} %copy-done, f32[2,16,128,128]{3,2,1,0:T(8,128)S(1)} %reshape.76, f32[128,128]{1,0:T(8,128)S(1)} %get-tuple-element.10, f32[128,128]{1,0:T(8,128)S(1)} %get-tuple-element.9, ...), kind=kOutput, calls=%fused_computation.27 | convolution fusion | flops 808157184 | bytes 8585216 | tf_op jit(solution)/shard_map/rsak,az->rszk/dot_general | solution.py:19
  109.4 2.3 %convolution_add_fusion = f32[128,2,16,128]{3,0,2,1:T(8,128)S(1)} fusion(f32[128,2,16,128]{3,0,2,1:T(8,128)S(1)} %fusion.26, f32[2,16,128,128]{3,2,1,0:T(8,128)S(1)} %copy-done, f32[2,16,128,128]{3,2,1,0:T(8,128)S(1)} %reshape.76, f32[128,128]{1,0:T(8,128)S(1)} %get-tuple-element.10, f32[128,128]{1,0:T(8,128)S(1)} %get-tuple-element.9, ...), kind=kOutput, calls=%fused_computation.26 | convolution fusion | flops 808157184 | bytes 8585216 | tf_op jit(solution)/shard_map/rsak,az->rszk/dot_general | solution.py:19
  111.8 2.2 %fusion.10 = f32[128,2,16,128]{3,0,2,1:T(8,128)S(1)} fusion(f32[128,2,16,128]{3,0,2,1:T(8,128)S(1)} %convolution_add_fusion, f32[128,2,16,128]{3,0,2,1:T(8,128)S(1)} %convolution_subtract_fusion, f32[128,128]{1,0:T(8,128)S(1)} %copy.45, f32[128,128]{1,0:T(8,128)S(1)} %copy.44), kind=kOutput, calls=%fused_computation.14 | convolution fusion | flops 807124992 | bytes 6422528 | tf_op jit(solution)/shard_map/rszk,kt->trsz/dot_general | solution.py:19
  114.0 2.6 %fusion.20 = bf16[128,1,2,16,128]{4,0,3,2,1:T(8,128)(2,1)S(1)} fusion(f32[128,2,16,128]{3,0,2,1:T(8,128)S(1)} %fusion.10, f32[128,2,16,128]{3,0,2,1:T(8,128)S(1)} %convolution_add_fusion, f32[128,2,16,128]{3,0,2,1:T(8,128)S(1)} %convolution_subtract_fusion, f32[128,128]{1,0:T(8,128)S(1)} %copy.45, f32[128,128]{1,0:T(8,128)S(1)} %copy.44), kind=kOutput, calls=%fused_computation.28 | convolution fusion | flops 808173568 | bytes 7471104 | tf_op jit(solution)/shard_map/rszk,kt->trsz/dot_general | solution.py:19
  116.6 2.2 %fusion.8 = f32[128,2,16,128]{3,0,2,1:T(8,128)S(1)} fusion(f32[128,2,16,128]{3,0,2,1:T(8,128)S(1)} %convolution_add_fusion, f32[128,2,16,128]{3,0,2,1:T(8,128)S(1)} %convolution_subtract_fusion, f32[128,128]{1,0:T(8,128)S(1)} %copy.45, f32[128,128]{1,0:T(8,128)S(1)} %copy.44), kind=kOutput, calls=%fused_computation.12 | convolution fusion | flops 807124992 | bytes 6422528 | tf_op jit(solution)/shard_map/rszk,kt->trsz/dot_general | solution.py:19
  118.8 2.4 %fusion.23 = bf16[128,1,2,16,128]{4,0,3,2,1:T(8,128)(2,1)S(1)} fusion(f32[128,2,16,128]{3,0,2,1:T(8,128)S(1)} %fusion.8, f32[128,2,16,128]{3,0,2,1:T(8,128)S(1)} %convolution_add_fusion, f32[128,2,16,128]{3,0,2,1:T(8,128)S(1)} %convolution_subtract_fusion, f32[128,128]{1,0:T(8,128)S(1)} %copy.45, f32[128,128]{1,0:T(8,128)S(1)} %copy.44), kind=kOutput, calls=%fused_computation.29 | convolution fusion | flops 808173568 | bytes 7471104 | tf_op jit(solution)/shard_map/rszk,kt->trsz/dot_general | solution.py:19
  122.8 52.0 %all_to_all.10 = bf16[128,2,2,16,128]{4,3,2,1,0:T(8,128)(2,1)S(1)} all-to-all(bf16[128,2,2,16,128]{4,3,2,1,0:T(8,128)(2,1)S(1)} %copy.46), channel_id=1, replica_groups=mesh['wave'=8,'pix'=16] {'wave','pix'}, dimensions={0} | all-to-all | bytes 4194304 | tf_op jit(solution)/shard_map/all_to_all | solution.py:69
  176.0 5.9 %fusion.1 = f32[2,128,2048]{2,1,0:T(8,128)S(1)} fusion(bf16[2,128,2048]{1,2,0:T(8,128)(2,1)S(1)} %bitcast.97, bf16[2,2048,2048]{2,1,0:T(8,128)(2,1)} %all-gather.2.cloned.1.call-done), kind=kOutput, calls=%fused_computation.3 | convolution fusion | flops 2147483648 | bytes 11534336 | tf_op jit(solution)/shard_map/dot_general | solution.py:75
  181.9 6.5 %fusion = f32[2,128,2048]{2,1,0:T(8,128)S(1)} fusion(bf16[2,128,2048]{1,2,0:T(8,128)(2,1)S(1)} %bitcast.99, bf16[2,2048,2048]{2,1,0:T(8,128)(2,1)} %all-gather.2.cloned.1.call-done), kind=kOutput, calls=%fused_computation.2 | convolution fusion | flops 2147483648 | bytes 11534336 | tf_op jit(solution)/shard_map/dot_general | solution.py:80
  188.4 2.4 %fusion.5 = f32[1,2,128,2048]{3,2,1,0:T(8,128)S(1)} fusion(f32[2,128,2048]{2,1,0:T(8,128)S(1)} %fusion.1, bf16[2,128,2048]{1,2,0:T(8,128)(2,1)S(1)} %bitcast.100, bf16[2,2048,2048]{2,1,0:T(8,128)(2,1)S(1)} %copy-done.1), kind=kOutput, calls=%fused_computation.8 | convolution fusion | flops 2148007936 | bytes 13631488 | tf_op jit(solution)/shard_map/dot_general | solution.py:77
  190.8 2.4 %fusion.7 = f32[1,2,128,2048]{3,2,1,0:T(8,128)S(1)} fusion(f32[2,128,2048]{2,1,0:T(8,128)S(1)} %fusion, bf16[2,128,2048]{1,2,0:T(8,128)(2,1)S(1)} %bitcast.98, bf16[2,2048,2048]{2,1,0:T(8,128)(2,1)S(1)} %copy-done.1), kind=kOutput, calls=%fused_computation.10 | convolution fusion | flops 2148007936 | bytes 13631488 | tf_op jit(solution)/shard_map/dot_general | solution.py:78
  193.2 2.3 %pad_maximum_fusion = f32[2,2,128,2048]{3,2,1,0:T(8,128)} fusion(f32[1,2,128,2048]{3,2,1,0:T(8,128)S(1)} %fusion.7, f32[1,2,128,2048]{3,2,1,0:T(8,128)S(1)} %fusion.5), kind=kLoop, calls=%fused_computation.6 | loop fusion | flops 1048576 | bytes 8388608 | tf_op jit(solution)/shard_map/stack | solution.py:81
  (22 shorter events, 4.3 us)
Async XLA Ops:
  6.5 169.5 %all-gather.2.cloned.1.call-start = ((), (), s32[]{:S(2)}) async-start(), calls=%async_computation.2 | async-start | bytes 17825792 | tf_op jit(solution)/shard_map/all_gather | solution.py:74
  11.7 7.2 %copy-start.2 = (f32[2048]{0:T(1024)S(1)}, f32[2048]{0:T(1024)}, u32[]{:S(2)}) copy-start(f32[2048]{0:T(1024)} %param.6) | copy-start | bytes 24580
  11.7 53.0 %copy-start.3 = (f32[2048]{0:T(1024)S(1)}, f32[2048]{0:T(1024)}, u32[]{:S(2)}) copy-start(f32[2048]{0:T(1024)} %param.5) | copy-start | bytes 24580
  11.7 76.2 %all-to-all-start = ((bf16[8,2,2,16,2048]{4,3,2,1,0:T(8,128)(2,1)}), bf16[8,2,2,16,2048]{4,3,2,1,0:T(8,128)(2,1)S(1)}, u32[]{:S(2)}, u32[]{:S(2)}) async-start(bf16[8,2,2,16,2048]{4,3,2,1,0:T(8,128)(2,1)} %copy.41), calls=%async_computation | async-start | bytes 4194304 | tf_op jit(solution)/shard_map/all_to_all | solution.py:38
  100.6 4.1 %copy-start = (f32[2,16,128,128]{3,2,1,0:T(8,128)S(1)}, f32[2,16,128,128]{3,2,1,0:T(8,128)}, u32[]{:S(2)}) copy-start(f32[2,16,128,128]{3,2,1,0:T(8,128)} %reshape.77) | copy-start | bytes 6291460
  176.0 12.4 %copy-start.1 = (bf16[2,2048,2048]{2,1,0:T(8,128)(2,1)S(1)}, bf16[2,2048,2048]{2,1,0:T(8,128)(2,1)}, u32[]{:S(2)}) copy-start(bf16[2,2048,2048]{2,1,0:T(8,128)(2,1)} %all-gather.2.cloned.1.call-done) | copy-start | bytes 50331652
Sparse Core Ops, SparseCore 0:
  9.6 154.3 all-gather.1

commit v2 on v1

--- a/solution.py
+++ b/solution.py
@@ -36,8 +36,12 @@
     pieces = raw_spectra.reshape(2, row_count, wave_span, wave_count, sub_pix)
     pieces = jnp.transpose(pieces, (3, 0, 1, 4, 2))
     pieces = lax.all_to_all(pieces, "wave", 0, 0, tiled=True)
-    full_background = lax.all_gather(background, "wave", tiled=True)
-    full_dispersion = lax.all_gather(dispersion, "wave", tiled=True)
+    tables = jnp.broadcast_to(
+        jnp.stack((background, dispersion))[None], (wave_count, 2, wave_span)
+    )
+    tables = lax.all_to_all(tables, "wave", 0, 0, tiled=True)
+    full_background = tables[:, 0].reshape(length)
+    full_dispersion = tables[:, 1].reshape(length)
 
     spectra = jnp.transpose(pieces, (1, 2, 3, 0, 4)).reshape(2, row_count, sub_pix, length)
     real_part = spectra[0].astype(jnp.float32) - full_background

time: 203 us -> 207 us (1.020)
  blocking collectives: 121 us -> 40.8 us
  waiting for transfers between devices: 0.73 us -> 77.3 us
  starting transfers between devices: 6.51 us -> 10.7 us
  local copies, waits for them, and re-layouts: 18.4 us -> 20.8 us
    all_gather x2 -> x0, blocking collectives: 68.7 us -> none  [the longest x1 45.8 us: on_device(): full_dispersion = lax.all_gather(dispersion, 'wave', tiled=True)]
    all_gather x1, waiting for transfers between devices: 0.02 us -> 48.5 us  [on_device(): column_piece = lax.all_gather(propagator, 'pix', axis=2, tiled=True)]
    all_to_all x1, waiting for transfers between devices: 0.01 us -> 27.2 us  [on_device(): pieces = lax.all_to_all(pieces, 'wave', 0, 0, tiled=True)]
    all_to_all x1, blocking collectives: 52 us -> 40.8 us  [on_device(): arrived = lax.all_to_all(depth_bf, ('wave', 'pix'), 0, 0, tiled=True)]
    all_to_all x0 -> x1, starting transfers between devices: none -> 6.37 us  [on_device(): tables = lax.all_to_all(tables, 'wave', 0, 0, tiled=True)]
    all_to_all x1, starting transfers between devices: 6.51 us -> 4.28 us  [on_device(): pieces = lax.all_to_all(pieces, 'wave', 0, 0, tiled=True)]
  transfers between devices with their start and end apart: 2 -> 3, of which waited for: 0 -> 3; matrix products, arithmetic and copies ran while one was open for 20% -> 22% of each run, Pallas kernels for 0% -> 0%
where the time goes in v2:
time: 207 us; the launch traced here: 206 us
  waiting for transfers between devices  77.3 us (37%)
  blocking collectives  40.8 us (20%)
  matrix products  37.6 us (18%)
  local copies, waits for them, and re-layouts  20.8 us (10%)
  between operations  13.6 us (7%)
  starting transfers between devices  10.7 us (5%)
  other arithmetic  5.39 us (3%)
    all_gather x1, waiting for transfers between devices, on_device(): column_piece = lax.all_gather(propagator, 'pix', axis=2, tiled=True)  48.5 us
    all_to_all x1, blocking collectives, on_device(): arrived = lax.all_to_all(depth_bf, ('wave', 'pix'), 0, 0, tiled=True)  40.8 us
    all_to_all x1, waiting for transfers between devices, on_device(): pieces = lax.all_to_all(pieces, 'wave', 0, 0, tiled=True)  27.2 us
    dot_general x8, matrix products, dot(): return jnp.einsum(spec, a, b, precision=HIGHEST_PRECISION)  20.5 us
    convert_element_type x2, local copies, waits for them, and re-layouts, on_device(): imag_part = spectra[1].astype(jnp.float32)  6.86 us
    dot_general x1, matrix products, on_device(): jnp.dot(depth_field[1], column_piece[0], preferred_element_type=jnp.float32)  6.48 us
    all_to_all x1, starting transfers between devices, on_device(): tables = lax.all_to_all(tables, 'wave', 0, 0, tiled=True)  6.37 us
    dot_general x1, matrix products, on_device(): jnp.dot(depth_field[0], column_piece[0], preferred_element_type=jnp.float32)  5.87 us
  transfers between devices with their start and end apart: 3, of which 3 were waited for; matrix products, arithmetic and copies ran while one was open for 22% of the time, Pallas kernels for 0%

profile of v2, /device:TPU:1, one launch (start us, length us, event | category | flops | bytes accessed | tf_op | source)
XLA Modules:
  0.0 206.2 jit_solution(17094072000628537716)
XLA Ops:
  8.7 6.4 %all-to-all-start.1 = ((f32[8,2,2048]{2,1,0:T(2,128)}), f32[8,2,2048]{2,1,0:T(2,128)S(1)}, u32[]{:S(2)}, u32[]{:S(2)}) async-start(f32[8,2,2048]{2,1,0:T(2,128)} %broadcast_in_dim.2), calls=%async_computation.1 | async-start | bytes 262144 | tf_op jit(solution)/shard_map/all_to_all | solution.py:42
  15.0 2.9 %copy.40 = bf16[2,2,2048,128]{2,3,1,0:T(8,128)(2,1)S(1)} copy(bf16[2,2,2048,128]{3,2,1,0:T(8,128)(2,1)} %param.4) | data formatting | bytes 4194304 | tf_op args[0]
  20.3 4.3 %all-to-all-start = ((bf16[8,2,2,16,2048]{4,3,2,1,0:T(8,128)(2,1)}), bf16[8,2,2,16,2048]{4,3,2,1,0:T(8,128)(2,1)S(1)}, u32[]{:S(2)}, u32[]{:S(2)}) async-start(bf16[8,2,2,16,2048]{4,3,2,1,0:T(8,128)(2,1)} %copy.41), calls=%async_computation | async-start | bytes 4194304 | tf_op jit(solution)/shard_map/all_to_all | solution.py:38
  25.3 1.9 fusion.104
  27.3 27.2 %all-to-all-done = bf16[8,2,2,16,2048]{4,3,2,1,0:T(8,128)(2,1)S(1)} async-done(((bf16[8,2,2,16,2048]{4,3,2,1,0:T(8,128)(2,1)}), bf16[8,2,2,16,2048]{4,3,2,1,0:T(8,128)(2,1)S(1)}, u32[]{:S(2)}, u32[]{:S(2)}) %all-to-all-start) | async-done | bytes 2097184 | tf_op jit(solution)/shard_map/all_to_all | solution.py:38
  56.2 2.5 %copy.42 = f32[1,2,16,8,2048]{4,3,2,1,0:T(8,128)} copy(f32[1,2,16,8,2048]{4,2,1,0,3:T(8,128)S(1)} %get-tuple-element.7) | data formatting | bytes 4194304 | tf_op jit(solution)/shard_map/convert_element_type | solution.py:47
  58.7 1.7 reshape.90
  60.4 4.1 %copy.43 = f32[1,2,16,8,2048]{4,3,2,1,0:T(8,128)} copy(f32[1,2,16,8,2048]{4,2,1,0,3:T(8,128)} %get-tuple-element.8) | data formatting | bytes 4194304 | tf_op jit(solution)/shard_map/convert_element_type | solution.py:48
  64.6 2.7 %reshape.91 = f32[2,16,128,128]{3,2,1,0:T(8,128)} reshape(f32[1,2,16,8,2048]{4,3,2,1,0:T(8,128)} %copy.43) | data formatting | bytes 4194304 | tf_op jit(solution)/shard_map/convert_element_type | solution.py:48
  67.3 4.1 %fusion.27 = f32[128,2,16,128]{3,0,2,1:T(8,128)S(1)} fusion(f32[2,16,128,128]{3,2,1,0:T(8,128)} %reshape.91, f32[2,16,128,128]{3,2,1,0:T(8,128)S(1)} %reshape.90, f32[128,128]{1,0:T(8,128)S(1)} %bitcast.105, f32[128,128]{1,0:T(8,128)S(1)} %bitcast.109, f32[128,128]{1,0:T(8,128)S(1)} %bitcast.101), kind=kOutput, calls=%fused_computation.33 | convolution fusion | flops 807632896 | bytes 6488064 | tf_op jit(solution)/shard_map/rsak,az->rszk/dot_general | solution.py:19
  71.4 2.3 %fusion.26 = f32[128,2,16,128]{3,0,2,1:T(8,128)S(1)} fusion(f32[2,16,128,128]{3,2,1,0:T(8,128)S(1)} %copy-done, f32[2,16,128,128]{3,2,1,0:T(8,128)S(1)} %reshape.90, f32[128,128]{1,0:T(8,128)S(1)} %bitcast.106, f32[128,128]{1,0:T(8,128)S(1)} %bitcast.110, f32[128,128]{1,0:T(8,128)S(1)} %bitcast.102), kind=kOutput, calls=%fused_computation.32 | convolution fusion | flops 807632896 | bytes 6488064 | tf_op jit(solution)/shard_map/rsak,az->rszk/dot_general | solution.py:19
  73.7 2.3 %convolution_subtract_fusion = f32[128,2,16,128]{3,0,2,1:T(8,128)S(1)} fusion(f32[128,2,16,128]{3,0,2,1:T(8,128)S(1)} %fusion.27, f32[2,16,128,128]{3,2,1,0:T(8,128)S(1)} %copy-done, f32[2,16,128,128]{3,2,1,0:T(8,128)S(1)} %reshape.90, f32[128,128]{1,0:T(8,128)S(1)} %bitcast.107, f32[128,128]{1,0:T(8,128)S(1)} %bitcast.111, f32[128,128]{1,0:T(8,128)S(1)} %bitcast.103), kind=kOutput, calls=%fused_computation.27 | convolution fusion | flops 808157184 | bytes 8585216 | tf_op jit(solution)/shard_map/rsak,az->rszk/dot_general | solution.py:19
  76.1 2.3 %convolution_add_fusion = f32[128,2,16,128]{3,0,2,1:T(8,128)S(1)} fusion(f32[128,2,16,128]{3,0,2,1:T(8,128)S(1)} %fusion.26, f32[2,16,128,128]{3,2,1,0:T(8,128)S(1)} %copy-done, f32[2,16,128,128]{3,2,1,0:T(8,128)S(1)} %reshape.90, f32[128,128]{1,0:T(8,128)S(1)} %bitcast.108, f32[128,128]{1,0:T(8,128)S(1)} %bitcast.112, f32[128,128]{1,0:T(8,128)S(1)} %bitcast.104), kind=kOutput, calls=%fused_computation.26 | convolution fusion | flops 808157184 | bytes 8585216 | tf_op jit(solution)/shard_map/rsak,az->rszk/dot_general | solution.py:19
  78.4 2.2 %fusion.10 = f32[128,2,16,128]{3,0,2,1:T(8,128)S(1)} fusion(f32[128,2,16,128]{3,0,2,1:T(8,128)S(1)} %convolution_add_fusion, f32[128,2,16,128]{3,0,2,1:T(8,128)S(1)} %convolution_subtract_fusion, f32[128,128]{1,0:T(8,128)S(1)} %copy.45, f32[128,128]{1,0:T(8,128)S(1)} %copy.44), kind=kOutput, calls=%fused_computation.14 | convolution fusion | flops 807124992 | bytes 6422528 | tf_op jit(solution)/shard_map/rszk,kt->trsz/dot_general | solution.py:19
  80.7 2.6 %fusion.20 = bf16[128,1,2,16,128]{4,0,3,2,1:T(8,128)(2,1)S(1)} fusion(f32[128,2,16,128]{3,0,2,1:T(8,128)S(1)} %fusion.10, f32[128,2,16,128]{3,0,2,1:T(8,128)S(1)} %convolution_add_fusion, f32[128,2,16,128]{3,0,2,1:T(8,128)S(1)} %convolution_subtract_fusion, f32[128,128]{1,0:T(8,128)S(1)} %copy.45, f32[128,128]{1,0:T(8,128)S(1)} %copy.44), kind=kOutput, calls=%fused_computation.28 | convolution fusion | flops 808173568 | bytes 7471104 | tf_op jit(solution)/shard_map/rszk,kt->trsz/dot_general | solution.py:19
  83.3 2.2 %fusion.8 = f32[128,2,16,128]{3,0,2,1:T(8,128)S(1)} fusion(f32[128,2,16,128]{3,0,2,1:T(8,128)S(1)} %convolution_add_fusion, f32[128,2,16,128]{3,0,2,1:T(8,128)S(1)} %convolution_subtract_fusion, f32[128,128]{1,0:T(8,128)S(1)} %copy.45, f32[128,128]{1,0:T(8,128)S(1)} %copy.44), kind=kOutput, calls=%fused_computation.12 | convolution fusion | flops 807124992 | bytes 6422528 | tf_op jit(solution)/shard_map/rszk,kt->trsz/dot_general | solution.py:19
  85.5 2.4 %fusion.23 = bf16[128,1,2,16,128]{4,0,3,2,1:T(8,128)(2,1)S(1)} fusion(f32[128,2,16,128]{3,0,2,1:T(8,128)S(1)} %fusion.8, f32[128,2,16,128]{3,0,2,1:T(8,128)S(1)} %convolution_add_fusion, f32[128,2,16,128]{3,0,2,1:T(8,128)S(1)} %convolution_subtract_fusion, f32[128,128]{1,0:T(8,128)S(1)} %copy.45, f32[128,128]{1,0:T(8,128)S(1)} %copy.44), kind=kOutput, calls=%fused_computation.29 | convolution fusion | flops 808173568 | bytes 7471104 | tf_op jit(solution)/shard_map/rszk,kt->trsz/dot_general | solution.py:19
  89.5 40.8 %all_to_all.15 = bf16[128,2,2,16,128]{4,3,2,1,0:T(8,128)(2,1)S(1)} all-to-all(bf16[128,2,2,16,128]{4,3,2,1,0:T(8,128)(2,1)S(1)} %copy.46), channel_id=1, replica_groups=mesh['wave'=8,'pix'=16] {'wave','pix'}, dimensions={0} | all-to-all | bytes 4194304 | tf_op jit(solution)/shard_map/all_to_all | solution.py:73
  131.4 48.5 %all-gather.2.cloned.1.call-done = bf16[2,2048,2048]{2,1,0:T(8,128)(2,1)} async-done(((bf16[2,2048,128]{2,1,0:T(8,128)(2,1)}), bf16[2,2048,2048]{2,1,0:T(8,128)(2,1)}) %all-gather.2.cloned.1.call-update) | async-done | bytes 16777232 | tf_op jit(solution)/shard_map/all_gather | solution.py:78
  180.0 5.9 %fusion.1 = f32[2,128,2048]{2,1,0:T(8,128)S(1)} fusion(bf16[2,128,2048]{1,2,0:T(8,128)(2,1)S(1)} %bitcast.97, bf16[2,2048,2048]{2,1,0:T(8,128)(2,1)} %all-gather.2.cloned.1.call-done), kind=kOutput, calls=%fused_computation.3 | convolution fusion | flops 2147483648 | bytes 11534336 | tf_op jit(solution)/shard_map/dot_general | solution.py:79
  185.8 6.5 %fusion = f32[2,128,2048]{2,1,0:T(8,128)S(1)} fusion(bf16[2,128,2048]{1,2,0:T(8,128)(2,1)S(1)} %bitcast.99, bf16[2,2048,2048]{2,1,0:T(8,128)(2,1)} %all-gather.2.cloned.1.call-done), kind=kOutput, calls=%fused_computation.2 | convolution fusion | flops 2147483648 | bytes 11534336 | tf_op jit(solution)/shard_map/dot_general | solution.py:84
  192.3 2.4 %fusion.5 = f32[1,2,128,2048]{3,2,1,0:T(8,128)S(1)} fusion(f32[2,128,2048]{2,1,0:T(8,128)S(1)} %fusion.1, bf16[2,128,2048]{1,2,0:T(8,128)(2,1)S(1)} %bitcast.100, bf16[2,2048,2048]{2,1,0:T(8,128)(2,1)S(1)} %copy-done.1), kind=kOutput, calls=%fused_computation.8 | convolution fusion | flops 2148007936 | bytes 13631488 | tf_op jit(solution)/shard_map/dot_general | solution.py:81
  194.7 2.4 %fusion.7 = f32[1,2,128,2048]{3,2,1,0:T(8,128)S(1)} fusion(f32[2,128,2048]{2,1,0:T(8,128)S(1)} %fusion, bf16[2,128,2048]{1,2,0:T(8,128)(2,1)S(1)} %bitcast.98, bf16[2,2048,2048]{2,1,0:T(8,128)(2,1)S(1)} %copy-done.1), kind=kOutput, calls=%fused_computation.10 | convolution fusion | flops 2148007936 | bytes 13631488 | tf_op jit(solution)/shard_map/dot_general | solution.py:82
  197.1 2.3 %pad_maximum_fusion = f32[2,2,128,2048]{3,2,1,0:T(8,128)} fusion(f32[1,2,128,2048]{3,2,1,0:T(8,128)S(1)} %fusion.7, f32[1,2,128,2048]{3,2,1,0:T(8,128)S(1)} %fusion.5), kind=kLoop, calls=%fused_computation.6 | loop fusion | flops 1048576 | bytes 8388608 | tf_op jit(solution)/shard_map/stack | solution.py:85
  (20 shorter events, 9.5 us)
Async XLA Ops:
  6.5 173.4 %all-gather.2.cloned.1.call-start = ((), (), s32[]{:S(2)}) async-start(), calls=%async_computation.3 | async-start | bytes 17825792 | tf_op jit(solution)/shard_map/all_gather | solution.py:78
  8.7 11.6 %all-to-all-start.1 = ((f32[8,2,2048]{2,1,0:T(2,128)}), f32[8,2,2048]{2,1,0:T(2,128)S(1)}, u32[]{:S(2)}, u32[]{:S(2)}) async-start(f32[8,2,2048]{2,1,0:T(2,128)} %broadcast_in_dim.2), calls=%async_computation.1 | async-start | bytes 262144 | tf_op jit(solution)/shard_map/all_to_all | solution.py:42
  20.3 34.2 %all-to-all-start = ((bf16[8,2,2,16,2048]{4,3,2,1,0:T(8,128)(2,1)}), bf16[8,2,2,16,2048]{4,3,2,1,0:T(8,128)(2,1)S(1)}, u32[]{:S(2)}, u32[]{:S(2)}) async-start(bf16[8,2,2,16,2048]{4,3,2,1,0:T(8,128)(2,1)} %copy.41), calls=%async_computation | async-start | bytes 4194304 | tf_op jit(solution)/shard_map/all_to_all | solution.py:38
  67.3 4.1 %copy-start = (f32[2,16,128,128]{3,2,1,0:T(8,128)S(1)}, f32[2,16,128,128]{3,2,1,0:T(8,128)}, u32[]{:S(2)}) copy-start(f32[2,16,128,128]{3,2,1,0:T(8,128)} %reshape.91) | copy-start | bytes 6291460
  180.0 12.4 %copy-start.1 = (bf16[2,2048,2048]{2,1,0:T(8,128)(2,1)S(1)}, bf16[2,2048,2048]{2,1,0:T(8,128)(2,1)}, u32[]{:S(2)}) copy-start(bf16[2,2048,2048]{2,1,0:T(8,128)(2,1)} %all-gather.2.cloned.1.call-done) | copy-start | bytes 50331652
Sparse Core Ops, SparseCore 0:
  9.6 170.3 all-gather.1

commit v3 on v2

--- a/solution.py
+++ b/solution.py
@@ -75,13 +75,23 @@
     depth_field = jnp.transpose(arrived, (2, 3, 5, 1, 0, 4)).reshape(
         2, row_count, first, pix_count * pix_local
     )
-    column_piece = lax.all_gather(propagator, "pix", axis=2, tiled=True)
-    image_real = jnp.dot(
-        depth_field[0], column_piece[0], preferred_element_type=jnp.float32
-    ) - jnp.dot(depth_field[1], column_piece[1], preferred_element_type=jnp.float32)
-    image_imag = jnp.dot(
-        depth_field[0], column_piece[1], preferred_element_type=jnp.float32
-    ) + jnp.dot(depth_field[1], column_piece[0], preferred_element_type=jnp.float32)
+    halves = 2
+    half_rows = propagator.shape[1] // halves
+    image_real = 0.0
+    image_imag = 0.0
+    for half in range(halves):
+        rows = slice(half * half_rows, (half + 1) * half_rows)
+        column_piece = lax.all_gather(propagator[:, rows], "pix", axis=2, tiled=True)
+        depth_real = depth_field[0][:, :, rows]
+        depth_imag = depth_field[1][:, :, rows]
+        image_real = image_real + (
+            jnp.dot(depth_real, column_piece[0], preferred_element_type=jnp.float32)
+            - jnp.dot(depth_imag, column_piece[1], preferred_element_type=jnp.float32)
+        )
+        image_imag = image_imag + (
+            jnp.dot(depth_real, column_piece[1], preferred_element_type=jnp.float32)
+            + jnp.dot(depth_imag, column_piece[0], preferred_element_type=jnp.float32)
+        )
     return jnp.stack((image_real, image_imag))
 
 

time: 207 us -> 228 us (1.10)
  waiting for transfers between devices: 77.3 us -> 93.7 us
  local copies, waits for them, and re-layouts: 20.8 us -> 24.9 us
    all_gather x1 -> x2, waiting for transfers between devices: 48.5 us -> 65.1 us  [on_device(): lax.all_gather(propagator[:, rows], 'pix', axis=2, tiled=True)]
    slice x3 -> x4, local copies, waits for them, and re-layouts: 1.11 us -> 3.4 us  [the longest x1 2.29 us: on_device(): propagator[:, rows]]
    unnamed x5 -> x17, local copies, waits for them, and re-layouts: 2.95 us -> 4.75 us
    dot_general x4 -> x8, matrix products: 17.1 us -> 18.6 us  [the longest x2 8.53 us: on_device(): jnp.dot(depth_real, column_piece[0], preferred_element_type=jnp.float32)]
  transfers between devices with their start and end apart: 3 -> 4, of which waited for: 3 -> 3; matrix products, arithmetic and copies ran while one was open for 22% -> 21% of each run, Pallas kernels for 0% -> 0%
where the time goes in v3:
time: 228 us
  waiting for transfers between devices  93.7 us (41%)
  blocking collectives  40.8 us (18%)
  matrix products  39.1 us (17%)
  local copies, waits for them, and re-layouts  24.9 us (11%)
  between operations  13.7 us (6%)
  starting transfers between devices  10.7 us (5%)
  other arithmetic  4.91 us (2%)
    all_gather x2, waiting for transfers between devices, on_device(): lax.all_gather(propagator[:, rows], 'pix', axis=2, tiled=True)  65.1 us
    all_to_all x1, blocking collectives, on_device(): arrived = lax.all_to_all(depth_bf, ('wave', 'pix'), 0, 0, tiled=True)  40.8 us
    all_to_all x1, waiting for transfers between devices, on_device(): pieces = lax.all_to_all(pieces, 'wave', 0, 0, tiled=True)  27.1 us
    dot_general x8, matrix products, dot(): return jnp.einsum(spec, a, b, precision=HIGHEST_PRECISION)  20.6 us
    dot_general x2, matrix products, on_device(): jnp.dot(depth_real, column_piece[0], preferred_element_type=jnp.float32)  8.53 us
    convert_element_type x2, local copies, waits for them, and re-layouts, on_device(): imag_part = spectra[1].astype(jnp.float32)  6.9 us
    all_to_all x1, starting transfers between devices, on_device(): tables = lax.all_to_all(tables, 'wave', 0, 0, tiled=True)  6.37 us
    dot_general x2, matrix products, on_device(): jnp.dot(depth_imag, column_piece[0], preferred_element_type=jnp.float32)  4.88 us
  transfers between devices with their start and end apart: 4, of which 3 were waited for; matrix products, arithmetic and copies ran while one was open for 21% of the time, Pallas kernels for 0%

profile of v3, /device:TPU:1, one launch (start us, length us, event | category | flops | bytes accessed | tf_op | source)
XLA Modules:
  0.0 227.8 jit_solution(7390063378028135990)
XLA Ops:
  6.5 2.3 %fusion.120 = (bf16[2,1024,128]{2,1,0:T(8,128)(2,1)}, bf16[2,1024,128]{2,1,0:T(8,128)(2,1)}) fusion(bf16[2,2048,128]{2,1,0:T(8,128)(2,1)} %param.7), kind=kLoop, calls=%fused_computation.129 | loop fusion | bytes 2097152 | tf_op jit(solution)/shard_map/slice | solution.py:84
  10.3 6.4 %all-to-all-start.1 = ((f32[8,2,2048]{2,1,0:T(2,128)}), f32[8,2,2048]{2,1,0:T(2,128)S(1)}, u32[]{:S(2)}, u32[]{:S(2)}) async-start(f32[8,2,2048]{2,1,0:T(2,128)} %broadcast_in_dim.2), calls=%async_computation.1 | async-start | bytes 262144 | tf_op jit(solution)/shard_map/all_to_all | solution.py:42
  16.7 2.9 %copy.40 = bf16[2,2,2048,128]{2,3,1,0:T(8,128)(2,1)S(1)} copy(bf16[2,2,2048,128]{3,2,1,0:T(8,128)(2,1)} %param.4) | data formatting | bytes 4194304 | tf_op args[0]
  22.0 4.3 %all-to-all-start = ((bf16[8,2,2,16,2048]{4,3,2,1,0:T(8,128)(2,1)}), bf16[8,2,2,16,2048]{4,3,2,1,0:T(8,128)(2,1)S(1)}, u32[]{:S(2)}, u32[]{:S(2)}) async-start(bf16[8,2,2,16,2048]{4,3,2,1,0:T(8,128)(2,1)} %copy.41), calls=%async_computation | async-start | bytes 4194304 | tf_op jit(solution)/shard_map/all_to_all | solution.py:38
  27.0 1.9 fusion.121
  28.9 27.1 %all-to-all-done = bf16[8,2,2,16,2048]{4,3,2,1,0:T(8,128)(2,1)S(1)} async-done(((bf16[8,2,2,16,2048]{4,3,2,1,0:T(8,128)(2,1)}), bf16[8,2,2,16,2048]{4,3,2,1,0:T(8,128)(2,1)S(1)}, u32[]{:S(2)}, u32[]{:S(2)}) %all-to-all-start) | async-done | bytes 2097184 | tf_op jit(solution)/shard_map/all_to_all | solution.py:38
  57.7 2.5 %copy.42 = f32[1,2,16,8,2048]{4,3,2,1,0:T(8,128)} copy(f32[1,2,16,8,2048]{4,2,1,0,3:T(8,128)S(1)} %get-tuple-element.7) | data formatting | bytes 4194304 | tf_op jit(solution)/shard_map/convert_element_type | solution.py:47
  60.2 1.7 reshape.90
  61.9 4.1 %copy.43 = f32[1,2,16,8,2048]{4,3,2,1,0:T(8,128)} copy(f32[1,2,16,8,2048]{4,2,1,0,3:T(8,128)} %get-tuple-element.8) | data formatting | bytes 4194304 | tf_op jit(solution)/shard_map/convert_element_type | solution.py:48
  66.1 2.8 %reshape.91 = f32[2,16,128,128]{3,2,1,0:T(8,128)} reshape(f32[1,2,16,8,2048]{4,3,2,1,0:T(8,128)} %copy.43) | data formatting | bytes 4194304 | tf_op jit(solution)/shard_map/convert_element_type | solution.py:48
  68.8 4.1 %fusion.43 = f32[128,2,16,128]{3,0,2,1:T(8,128)S(1)} fusion(f32[2,16,128,128]{3,2,1,0:T(8,128)} %reshape.91, f32[2,16,128,128]{3,2,1,0:T(8,128)S(1)} %reshape.90, f32[128,128]{1,0:T(8,128)S(1)} %bitcast.127, f32[128,128]{1,0:T(8,128)S(1)} %bitcast.131, f32[128,128]{1,0:T(8,128)S(1)} %bitcast.123), kind=kOutput, calls=%fused_computation.51 | convolution fusion | flops 807632896 | bytes 6488064 | tf_op jit(solution)/shard_map/rsak,az->rszk/dot_general | solution.py:19
  72.9 2.3 %fusion.42 = f32[128,2,16,128]{3,0,2,1:T(8,128)S(1)} fusion(f32[2,16,128,128]{3,2,1,0:T(8,128)S(1)} %copy-done, f32[2,16,128,128]{3,2,1,0:T(8,128)S(1)} %reshape.90, f32[128,128]{1,0:T(8,128)S(1)} %bitcast.128, f32[128,128]{1,0:T(8,128)S(1)} %bitcast.132, f32[128,128]{1,0:T(8,128)S(1)} %bitcast.124), kind=kOutput, calls=%fused_computation.50 | convolution fusion | flops 807632896 | bytes 6488064 | tf_op jit(solution)/shard_map/rsak,az->rszk/dot_general | solution.py:19
  75.3 2.3 %convolution_subtract_fusion = f32[128,2,16,128]{3,0,2,1:T(8,128)S(1)} fusion(f32[128,2,16,128]{3,0,2,1:T(8,128)S(1)} %fusion.43, f32[2,16,128,128]{3,2,1,0:T(8,128)S(1)} %copy-done, f32[2,16,128,128]{3,2,1,0:T(8,128)S(1)} %reshape.90, f32[128,128]{1,0:T(8,128)S(1)} %bitcast.129, f32[128,128]{1,0:T(8,128)S(1)} %bitcast.133, f32[128,128]{1,0:T(8,128)S(1)} %bitcast.125), kind=kOutput, calls=%fused_computation.37 | convolution fusion | flops 808157184 | bytes 8585216 | tf_op jit(solution)/shard_map/rsak,az->rszk/dot_general | solution.py:19
  77.6 2.4 %convolution_add_fusion = f32[128,2,16,128]{3,0,2,1:T(8,128)S(1)} fusion(f32[128,2,16,128]{3,0,2,1:T(8,128)S(1)} %fusion.42, f32[2,16,128,128]{3,2,1,0:T(8,128)S(1)} %copy-done, f32[2,16,128,128]{3,2,1,0:T(8,128)S(1)} %reshape.90, f32[128,128]{1,0:T(8,128)S(1)} %bitcast.130, f32[128,128]{1,0:T(8,128)S(1)} %bitcast.134, f32[128,128]{1,0:T(8,128)S(1)} %bitcast.126), kind=kOutput, calls=%fused_computation.36 | convolution fusion | flops 808157184 | bytes 8585216 | tf_op jit(solution)/shard_map/rsak,az->rszk/dot_general | solution.py:19
  80.0 2.2 fusion.18
  82.2 2.6 %fusion.28 = bf16[128,1,2,16,128]{4,0,3,2,1:T(8,128)(2,1)S(1)} fusion(f32[128,2,16,128]{3,0,2,1:T(8,128)S(1)} %fusion.18, f32[128,2,16,128]{3,0,2,1:T(8,128)S(1)} %convolution_add_fusion, f32[128,2,16,128]{3,0,2,1:T(8,128)S(1)} %convolution_subtract_fusion, f32[128,128]{1,0:T(8,128)S(1)} %copy.45, f32[128,128]{1,0:T(8,128)S(1)} %copy.44), kind=kOutput, calls=%fused_computation.38 | convolution fusion | flops 808173568 | bytes 7471104 | tf_op jit(solution)/shard_map/rszk,kt->trsz/dot_general | solution.py:19
  84.8 2.2 fusion.16
  87.1 2.4 %fusion.31 = bf16[128,1,2,16,128]{4,0,3,2,1:T(8,128)(2,1)S(1)} fusion(f32[128,2,16,128]{3,0,2,1:T(8,128)S(1)} %fusion.16, f32[128,2,16,128]{3,0,2,1:T(8,128)S(1)} %convolution_add_fusion, f32[128,2,16,128]{3,0,2,1:T(8,128)S(1)} %convolution_subtract_fusion, f32[128,128]{1,0:T(8,128)S(1)} %copy.45, f32[128,128]{1,0:T(8,128)S(1)} %copy.44), kind=kOutput, calls=%fused_computation.39 | convolution fusion | flops 808173568 | bytes 7471104 | tf_op jit(solution)/shard_map/rszk,kt->trsz/dot_general | solution.py:19
  91.0 40.8 %all_to_all.15 = bf16[128,2,2,16,128]{4,3,2,1,0:T(8,128)(2,1)S(1)} all-to-all(bf16[128,2,2,16,128]{4,3,2,1,0:T(8,128)(2,1)S(1)} %copy.46), channel_id=1, replica_groups=mesh['wave'=8,'pix'=16] {'wave','pix'}, dimensions={0} | all-to-all | bytes 4194304 | tf_op jit(solution)/shard_map/all_to_all | solution.py:73
  133.0 4.9 %fusion.5 = f32[2,128,2048]{2,1,0:T(8,128)} fusion(bf16[2,1024,2048]{2,1,0:T(8,128)(2,1)} %all-gather.5.cloned.1.call-done, bf16[2,128,2048]{1,2,0:T(8,128)(2,1)S(1)} %bitcast.112), kind=kOutput, calls=%fused_computation.10 | convolution fusion | flops 1073741824 | bytes 6815744 | tf_op jit(solution)/shard_map/dot_general | solution.py:88
  137.9 65.0 %all-gather.3.cloned.1.call-done = bf16[2,1024,2048]{2,1,0:T(8,128)(2,1)} async-done(((bf16[2,1024,128]{2,1,0:T(8,128)(2,1)}), bf16[2,1024,2048]{2,1,0:T(8,128)(2,1)}) %all-gather.3.cloned.1.call-update) | async-done | bytes 8388624 | tf_op jit(solution)/shard_map/all_gather | solution.py:84
  202.9 3.6 %fusion.1 = f32[2,128,2048]{2,1,0:T(8,128)S(1)} fusion(bf16[2,1024,2048]{2,1,0:T(8,128)(2,1)} %all-gather.3.cloned.1.call-done, bf16[2,128,2048]{1,2,0:T(8,128)(2,1)S(1)} %bitcast.113), kind=kOutput, calls=%fused_computation.6 | convolution fusion | flops 1073741824 | bytes 6815744 | tf_op jit(solution)/shard_map/dot_general | solution.py:88
  206.6 3.6 %fusion.4 = f32[2,128,2048]{2,1,0:T(8,128)S(1)} fusion(bf16[2,1024,2048]{2,1,0:T(8,128)(2,1)} %all-gather.5.cloned.1.call-done, bf16[2,128,2048]{1,2,0:T(8,128)(2,1)S(1)} %bitcast.116), kind=kOutput, calls=%fused_computation.9 | convolution fusion | flops 1073741824 | bytes 6815744 | tf_op jit(solution)/shard_map/dot_general | solution.py:93
  218.5 2.5 %pad_maximum_fusion = f32[2,2,128,2048]{3,2,1,0:T(8,128)} fusion(f32[1,2,128,2048]{3,2,1,0:T(8,128)S(1)} %fusion.13, f32[1,2,128,2048]{3,2,1,0:T(8,128)S(1)} %fusion.15), kind=kLoop, calls=%fused_computation.4 | loop fusion | flops 1048576 | bytes 8388608 | tf_op jit(solution)/shard_map/stack | solution.py:95
  (42 shorter events, 17.0 us)
Async XLA Ops:
  6.5 3.1 %copy-start.3 = (f32[2048]{0:T(1024)S(1)}, f32[2048]{0:T(1024)}, u32[]{:S(2)}) copy-start(f32[2048]{0:T(1024)} %param.5) | copy-start | bytes 24580
  6.5 3.1 %copy-start.2 = (f32[2048]{0:T(1024)S(1)}, f32[2048]{0:T(1024)}, u32[]{:S(2)}) copy-start(f32[2048]{0:T(1024)} %param.6) | copy-start | bytes 24580
  6.5 126.4 %all-gather.5.cloned.1.call-start = ((), (), s32[]{:S(2)}) async-start(), calls=%async_computation.4 | async-start | bytes 8912896 | tf_op jit(solution)/shard_map/all_gather | solution.py:84
  8.9 194.1 %all-gather.3.cloned.1.call-start = ((), (), s32[]{:S(2)}) async-start(), calls=%async_computation.3 | async-start | bytes 8912896 | tf_op jit(solution)/shard_map/all_gather | solution.py:84
  10.3 11.6 %all-to-all-start.1 = ((f32[8,2,2048]{2,1,0:T(2,128)}), f32[8,2,2048]{2,1,0:T(2,128)S(1)}, u32[]{:S(2)}, u32[]{:S(2)}) async-start(f32[8,2,2048]{2,1,0:T(2,128)} %broadcast_in_dim.2), calls=%async_computation.1 | async-start | bytes 262144 | tf_op jit(solution)/shard_map/all_to_all | solution.py:42
  22.0 34.0 %all-to-all-start = ((bf16[8,2,2,16,2048]{4,3,2,1,0:T(8,128)(2,1)}), bf16[8,2,2,16,2048]{4,3,2,1,0:T(8,128)(2,1)S(1)}, u32[]{:S(2)}, u32[]{:S(2)}) async-start(bf16[8,2,2,16,2048]{4,3,2,1,0:T(8,128)(2,1)} %copy.41), calls=%async_computation | async-start | bytes 4194304 | tf_op jit(solution)/shard_map/all_to_all | solution.py:38
  68.8 4.1 %copy-start = (f32[2,16,128,128]{3,2,1,0:T(8,128)S(1)}, f32[2,16,128,128]{3,2,1,0:T(8,128)}, u32[]{:S(2)}) copy-start(f32[2,16,128,128]{3,2,1,0:T(8,128)} %reshape.91) | copy-start | bytes 6291460
  202.9 7.2 %slice-start.2 = ((s8[8388608]{0:T(1024)(128)(4,1)}), s8[4194304]{0:T(1024)(128)(4,1)S(1)}, s32[]{:S(2)}) async-start(s8[8388608]{0:T(1024)(128)(4,1)} %bitcast.110), calls=%async_computation.7 | async-start | bytes 8388608
  206.5 3.6 %slice-start.3 = ((s8[8388608]{0:T(1024)(128)(4,1)}), s8[4194304]{0:T(1024)(128)(4,1)S(1)}, s32[]{:S(2)}) async-start(s8[8388608]{0:T(1024)(128)(4,1)} %bitcast.110), calls=%async_computation.8 | async-start | bytes 8388608
  206.6 5.0 %slice-start = ((s8[8388608]{0:T(1024)(128)(4,1)}), s8[4194304]{0:T(1024)(128)(4,1)S(1)}, s32[]{:S(2)}) async-start(s8[8388608]{0:T(1024)(128)(4,1)} %bitcast.108), calls=%async_computation.5 | async-start | bytes 8388608
  210.2 2.5 %slice-start.1 = ((s8[8388608]{0:T(1024)(128)(4,1)}), s8[4194304]{0:T(1024)(128)(4,1)S(1)}, s32[]{:S(2)}) async-start(s8[8388608]{0:T(1024)(128)(4,1)} %bitcast.108), calls=%async_computation.6 | async-start | bytes 8388608
  210.2 3.1 %copy-start.1 = (f32[2,128,2048]{2,1,0:T(8,128)S(1)}, f32[2,128,2048]{2,1,0:T(8,128)}, u32[]{:S(2)}) copy-start(f32[2,128,2048]{2,1,0:T(8,128)} %fusion.5) | copy-start | bytes 6291460
Sparse Core Ops, SparseCore 0:
  9.6 110.4 all-gather.4
  122.3 80.5 all-gather.2

commit v4 on v2

--- a/solution.py
+++ b/solution.py
@@ -76,13 +76,16 @@
         2, row_count, first, pix_count * pix_local
     )
     column_piece = lax.all_gather(propagator, "pix", axis=2, tiled=True)
-    image_real = jnp.dot(
-        depth_field[0], column_piece[0], preferred_element_type=jnp.float32
-    ) - jnp.dot(depth_field[1], column_piece[1], preferred_element_type=jnp.float32)
-    image_imag = jnp.dot(
-        depth_field[0], column_piece[1], preferred_element_type=jnp.float32
-    ) + jnp.dot(depth_field[1], column_piece[0], preferred_element_type=jnp.float32)
-    return jnp.stack((image_real, image_imag))
+    depth_real = depth_field[0]
+    depth_imag = depth_field[1]
+    left = jnp.stack(
+        (
+            jnp.concatenate((depth_real, -depth_imag), axis=-1),
+            jnp.concatenate((depth_imag, depth_real), axis=-1),
+        )
+    )
+    stacked = column_piece.reshape(2 * column_piece.shape[1], column_piece.shape[2])
+    return jnp.einsum("crzp,pq->crzq", left, stacked, preferred_element_type=jnp.float32)
 
 
 def solution(mesh):

time: 207 us -> 202 us (0.976)
  waiting for transfers between devices: 77.3 us -> 72.1 us
  local copies, waits for them, and re-layouts: 20.8 us -> 23.6 us
  matrix products: 37.6 us -> 35.4 us
    all_gather x1, waiting for transfers between devices: 48.5 us -> 43.2 us  [on_device(): column_piece = lax.all_gather(propagator, 'pix', axis=2, tiled=True)]
    dot_general x4 -> x1, matrix products: 17.1 us -> 14.9 us  [on_device(): jnp.einsum('crzp,pq->crzq', left, stacked, preferred_element_type=jnp.flo...]
  transfers between devices with their start and end apart: 3 -> 3, of which waited for: 3 -> 3; matrix products, arithmetic and copies ran while one was open for 22% -> 25% of each run, Pallas kernels for 0% -> 0%
where the time goes in v4:
time: 202 us
  waiting for transfers between devices  72.1 us (36%)
  blocking collectives  40.8 us (20%)
  matrix products  35.4 us (18%)
  local copies, waits for them, and re-layouts  23.6 us (12%)
  between operations  13.6 us (7%)
  starting transfers between devices  10.7 us (5%)
  other arithmetic  5.54 us (3%)
    all_gather x1, waiting for transfers between devices, on_device(): column_piece = lax.all_gather(propagator, 'pix', axis=2, tiled=True)  43.2 us
    all_to_all x1, blocking collectives, on_device(): arrived = lax.all_to_all(depth_bf, ('wave', 'pix'), 0, 0, tiled=True)  40.8 us
    all_to_all x1, waiting for transfers between devices, on_device(): pieces = lax.all_to_all(pieces, 'wave', 0, 0, tiled=True)  27.2 us
    dot_general x8, matrix products, dot(): return jnp.einsum(spec, a, b, precision=HIGHEST_PRECISION)  20.5 us
    dot_general x1, matrix products, on_device(): jnp.einsum('crzp,pq->crzq', left, stacked, preferred_element_type=jnp.flo...  14.9 us
    convert_element_type x2, local copies, waits for them, and re-layouts, on_device(): imag_part = spectra[1].astype(jnp.float32)  6.86 us
    all_to_all x1, starting transfers between devices, on_device(): tables = lax.all_to_all(tables, 'wave', 0, 0, tiled=True)  6.37 us
    all_to_all x1, starting transfers between devices, on_device(): pieces = lax.all_to_all(pieces, 'wave', 0, 0, tiled=True)  4.28 us
  transfers between devices with their start and end apart: 3, of which 3 were waited for; matrix products, arithmetic and copies ran while one was open for 25% of the time, Pallas kernels for 0%

profile of v4, /device:TPU:1, one launch (start us, length us, event | category | flops | bytes accessed | tf_op | source)
XLA Modules:
  0.0 201.7 jit_solution(1192183059728402671)
XLA Ops:
  8.7 6.4 %all-to-all-start.1 = ((f32[8,2,2048]{2,1,0:T(2,128)}), f32[8,2,2048]{2,1,0:T(2,128)S(1)}, u32[]{:S(2)}, u32[]{:S(2)}) async-start(f32[8,2,2048]{2,1,0:T(2,128)} %broadcast_in_dim.2), calls=%async_computation.1 | async-start | bytes 262144 | tf_op jit(solution)/shard_map/all_to_all | solution.py:42
  15.0 2.9 %copy.40 = bf16[2,2,2048,128]{2,3,1,0:T(8,128)(2,1)S(1)} copy(bf16[2,2,2048,128]{3,2,1,0:T(8,128)(2,1)} %param.4) | data formatting | bytes 4194304 | tf_op args[0]
  18.0 1.5 copy.41
  20.3 4.3 %all-to-all-start = ((bf16[8,2,2,16,2048]{4,3,2,1,0:T(8,128)(2,1)}), bf16[8,2,2,16,2048]{4,3,2,1,0:T(8,128)(2,1)S(1)}, u32[]{:S(2)}, u32[]{:S(2)}) async-start(bf16[8,2,2,16,2048]{4,3,2,1,0:T(8,128)(2,1)} %copy.41), calls=%async_computation | async-start | bytes 4194304 | tf_op jit(solution)/shard_map/all_to_all | solution.py:38
  25.3 1.9 fusion.101
  27.3 27.2 %all-to-all-done = bf16[8,2,2,16,2048]{4,3,2,1,0:T(8,128)(2,1)S(1)} async-done(((bf16[8,2,2,16,2048]{4,3,2,1,0:T(8,128)(2,1)}), bf16[8,2,2,16,2048]{4,3,2,1,0:T(8,128)(2,1)S(1)}, u32[]{:S(2)}, u32[]{:S(2)}) %all-to-all-start) | async-done | bytes 2097184 | tf_op jit(solution)/shard_map/all_to_all | solution.py:38
  54.5 1.7 slice_convert_fusion.1
  56.2 2.5 %copy.42 = f32[1,2,16,8,2048]{4,3,2,1,0:T(8,128)} copy(f32[1,2,16,8,2048]{4,2,1,0,3:T(8,128)S(1)} %get-tuple-element.7) | data formatting | bytes 4194304 | tf_op jit(solution)/shard_map/convert_element_type | solution.py:47
  58.7 1.7 reshape.94
  60.4 4.1 %copy.43 = f32[1,2,16,8,2048]{4,3,2,1,0:T(8,128)} copy(f32[1,2,16,8,2048]{4,2,1,0,3:T(8,128)} %get-tuple-element.8) | data formatting | bytes 4194304 | tf_op jit(solution)/shard_map/convert_element_type | solution.py:48
  64.6 2.7 %reshape.95 = f32[2,16,128,128]{3,2,1,0:T(8,128)} reshape(f32[1,2,16,8,2048]{4,3,2,1,0:T(8,128)} %copy.43) | data formatting | bytes 4194304 | tf_op jit(solution)/shard_map/convert_element_type | solution.py:48
  67.3 4.1 %fusion.23 = f32[128,2,16,128]{3,0,2,1:T(8,128)S(1)} fusion(f32[2,16,128,128]{3,2,1,0:T(8,128)} %reshape.95, f32[2,16,128,128]{3,2,1,0:T(8,128)S(1)} %reshape.94, f32[128,128]{1,0:T(8,128)S(1)} %bitcast.87, f32[128,128]{1,0:T(8,128)S(1)} %bitcast.91, f32[128,128]{1,0:T(8,128)S(1)} %bitcast.83), kind=kOutput, calls=%fused_computation.28 | convolution fusion | flops 807632896 | bytes 6488064 | tf_op jit(solution)/shard_map/rsak,az->rszk/dot_general | solution.py:19
  71.4 2.3 %fusion.22 = f32[128,2,16,128]{3,0,2,1:T(8,128)S(1)} fusion(f32[2,16,128,128]{3,2,1,0:T(8,128)S(1)} %copy-done, f32[2,16,128,128]{3,2,1,0:T(8,128)S(1)} %reshape.94, f32[128,128]{1,0:T(8,128)S(1)} %bitcast.88, f32[128,128]{1,0:T(8,128)S(1)} %bitcast.92, f32[128,128]{1,0:T(8,128)S(1)} %bitcast.84), kind=kOutput, calls=%fused_computation.27 | convolution fusion | flops 807632896 | bytes 6488064 | tf_op jit(solution)/shard_map/rsak,az->rszk/dot_general | solution.py:19
  73.7 2.3 %convolution_subtract_fusion = f32[128,2,16,128]{3,0,2,1:T(8,128)S(1)} fusion(f32[128,2,16,128]{3,0,2,1:T(8,128)S(1)} %fusion.23, f32[2,16,128,128]{3,2,1,0:T(8,128)S(1)} %copy-done, f32[2,16,128,128]{3,2,1,0:T(8,128)S(1)} %reshape.94, f32[128,128]{1,0:T(8,128)S(1)} %bitcast.89, f32[128,128]{1,0:T(8,128)S(1)} %bitcast.93, f32[128,128]{1,0:T(8,128)S(1)} %bitcast.85), kind=kOutput, calls=%fused_computation.22 | convolution fusion | flops 808157184 | bytes 8585216 | tf_op jit(solution)/shard_map/rsak,az->rszk/dot_general | solution.py:19
  76.1 2.3 %convolution_add_fusion = f32[128,2,16,128]{3,0,2,1:T(8,128)S(1)} fusion(f32[128,2,16,128]{3,0,2,1:T(8,128)S(1)} %fusion.22, f32[2,16,128,128]{3,2,1,0:T(8,128)S(1)} %copy-done, f32[2,16,128,128]{3,2,1,0:T(8,128)S(1)} %reshape.94, f32[128,128]{1,0:T(8,128)S(1)} %bitcast.90, f32[128,128]{1,0:T(8,128)S(1)} %bitcast.94, f32[128,128]{1,0:T(8,128)S(1)} %bitcast.86), kind=kOutput, calls=%fused_computation.21 | convolution fusion | flops 808157184 | bytes 8585216 | tf_op jit(solution)/shard_map/rsak,az->rszk/dot_general | solution.py:19
  78.4 2.2 %fusion.6 = f32[128,2,16,128]{3,0,2,1:T(8,128)S(1)} fusion(f32[128,2,16,128]{3,0,2,1:T(8,128)S(1)} %convolution_add_fusion, f32[128,2,16,128]{3,0,2,1:T(8,128)S(1)} %convolution_subtract_fusion, f32[128,128]{1,0:T(8,128)S(1)} %copy.45, f32[128,128]{1,0:T(8,128)S(1)} %copy.44), kind=kOutput, calls=%fused_computation.9 | convolution fusion | flops 807124992 | bytes 6422528 | tf_op jit(solution)/shard_map/rszk,kt->trsz/dot_general | solution.py:19
  80.7 2.6 %fusion.16 = bf16[128,1,2,16,128]{4,0,3,2,1:T(8,128)(2,1)S(1)} fusion(f32[128,2,16,128]{3,0,2,1:T(8,128)S(1)} %fusion.6, f32[128,2,16,128]{3,0,2,1:T(8,128)S(1)} %convolution_add_fusion, f32[128,2,16,128]{3,0,2,1:T(8,128)S(1)} %convolution_subtract_fusion, f32[128,128]{1,0:T(8,128)S(1)} %copy.45, f32[128,128]{1,0:T(8,128)S(1)} %copy.44), kind=kOutput, calls=%fused_computation.23 | convolution fusion | flops 808173568 | bytes 7471104 | tf_op jit(solution)/shard_map/rszk,kt->trsz/dot_general | solution.py:19
  83.3 2.2 %fusion.4 = f32[128,2,16,128]{3,0,2,1:T(8,128)S(1)} fusion(f32[128,2,16,128]{3,0,2,1:T(8,128)S(1)} %convolution_add_fusion, f32[128,2,16,128]{3,0,2,1:T(8,128)S(1)} %convolution_subtract_fusion, f32[128,128]{1,0:T(8,128)S(1)} %copy.45, f32[128,128]{1,0:T(8,128)S(1)} %copy.44), kind=kOutput, calls=%fused_computation.7 | convolution fusion | flops 807124992 | bytes 6422528 | tf_op jit(solution)/shard_map/rszk,kt->trsz/dot_general | solution.py:19
  85.5 2.4 %fusion.19 = bf16[128,1,2,16,128]{4,0,3,2,1:T(8,128)(2,1)S(1)} fusion(f32[128,2,16,128]{3,0,2,1:T(8,128)S(1)} %fusion.4, f32[128,2,16,128]{3,0,2,1:T(8,128)S(1)} %convolution_add_fusion, f32[128,2,16,128]{3,0,2,1:T(8,128)S(1)} %convolution_subtract_fusion, f32[128,128]{1,0:T(8,128)S(1)} %copy.45, f32[128,128]{1,0:T(8,128)S(1)} %copy.44), kind=kOutput, calls=%fused_computation.24 | convolution fusion | flops 808173568 | bytes 7471104 | tf_op jit(solution)/shard_map/rszk,kt->trsz/dot_general | solution.py:19
  89.5 40.8 %all_to_all.15 = bf16[128,2,2,16,128]{4,3,2,1,0:T(8,128)(2,1)S(1)} all-to-all(bf16[128,2,2,16,128]{4,3,2,1,0:T(8,128)(2,1)S(1)} %copy.46), channel_id=1, replica_groups=mesh['wave'=8,'pix'=16] {'wave','pix'}, dimensions={0} | all-to-all | bytes 4194304 | tf_op jit(solution)/shard_map/all_to_all | solution.py:73
  133.0 1.5 copy.50
  134.5 2.2 %maximum_bitcast_fusion = (bf16[1,2,128,4096]{3,2,1,0:T(8,128)(2,1)}, bf16[1,2,128,4096]{3,2,1,0:T(8,128)(2,1)}) fusion(bf16[2,128,2048]{2,1,0:T(8,128)(2,1)S(1)} %neg.3, bf16[2,128,2048]{2,1,0:T(8,128)(2,1)S(1)} %copy.50, bf16[2,128,2048]{2,1,0:T(8,128)(2,1)S(1)} %copy.49), kind=kLoop, calls=%fused_computation.5 | loop fusion | flops 8388608 | bytes 7340032 | tf_op jit(solution)/shard_map/stack | solution.py:81
  136.7 43.2 %all-gather.2.cloned.1.call-done = bf16[2,2048,2048]{2,1,0:T(8,128)(2,1)} async-done(((bf16[2,2048,128]{2,1,0:T(8,128)(2,1)}), bf16[2,2048,2048]{2,1,0:T(8,128)(2,1)}) %all-gather.2.cloned.1.call-update) | async-done | bytes 16777232 | tf_op jit(solution)/shard_map/all_gather | solution.py:78
  180.0 14.9 %fusion = f32[2,2,128,2048]{3,2,1,0:T(8,128)} fusion(bf16[4096,2048,1,1]{1,0,3,2:T(8,128)(2,1)} %bitcast.97, bf16[1,2,128,4096]{3,2,1,0:T(8,128)(2,1)} %get-tuple-element.10, bf16[1,2,128,4096]{3,2,1,0:T(8,128)(2,1)} %get-tuple-element.9), kind=kOutput, calls=%fused_computation | convolution fusion | flops 8592031744 | bytes 25165824 | tf_op jit(solution)/shard_map/crzp,pq->crzq/dot_general | solution.py:88
  (18 shorter events, 7.9 us)
Async XLA Ops:
  6.5 173.4 %all-gather.2.cloned.1.call-start = ((), (), s32[]{:S(2)}) async-start(), calls=%async_computation.3 | async-start | bytes 17825792 | tf_op jit(solution)/shard_map/all_gather | solution.py:78
  8.7 11.6 %all-to-all-start.1 = ((f32[8,2,2048]{2,1,0:T(2,128)}), f32[8,2,2048]{2,1,0:T(2,128)S(1)}, u32[]{:S(2)}, u32[]{:S(2)}) async-start(f32[8,2,2048]{2,1,0:T(2,128)} %broadcast_in_dim.2), calls=%async_computation.1 | async-start | bytes 262144 | tf_op jit(solution)/shard_map/all_to_all | solution.py:42
  20.3 34.2 %all-to-all-start = ((bf16[8,2,2,16,2048]{4,3,2,1,0:T(8,128)(2,1)}), bf16[8,2,2,16,2048]{4,3,2,1,0:T(8,128)(2,1)S(1)}, u32[]{:S(2)}, u32[]{:S(2)}) async-start(bf16[8,2,2,16,2048]{4,3,2,1,0:T(8,128)(2,1)} %copy.41), calls=%async_computation | async-start | bytes 4194304 | tf_op jit(solution)/shard_map/all_to_all | solution.py:38
  67.3 4.1 %copy-start = (f32[2,16,128,128]{3,2,1,0:T(8,128)S(1)}, f32[2,16,128,128]{3,2,1,0:T(8,128)}, u32[]{:S(2)}) copy-start(f32[2,16,128,128]{3,2,1,0:T(8,128)} %reshape.95) | copy-start | bytes 6291460
Sparse Core Ops, SparseCore 0:
  9.6 170.3 all-gather.1

commit v5 on v4

--- a/solution.py
+++ b/solution.py
@@ -5,7 +5,7 @@
 from jax import lax
 from jax.sharding import PartitionSpec as P
 
-HIGHEST_PRECISION = lax.Precision.HIGHEST
+MATMUL_PRECISION = lax.Precision.HIGH
 
 
 def twiddle_table(left_index, right_index, modulus, scale=1.0):
@@ -16,7 +16,7 @@
 
 def complex_contract(spec, real, imag, cosine, sine_part):
     def dot(a, b):
-        return jnp.einsum(spec, a, b, precision=HIGHEST_PRECISION)
+        return jnp.einsum(spec, a, b, precision=MATMUL_PRECISION)
 
     return (dot(real, cosine) - dot(imag, sine_part), dot(real, sine_part) + dot(imag, cosine))
 

time: 202 us -> 202 us (level)
  matrix products: 35.4 us -> 28 us
  waiting for transfers between devices: 72.1 us -> 79.3 us
    dot_general x8, matrix products: 20.5 us -> 13.1 us  [dot(): return jnp.einsum(spec, a, b, precision=MATMUL_PRECISION)]
    all_gather x1, waiting for transfers between devices: 43.2 us -> 50.4 us  [on_device(): column_piece = lax.all_gather(propagator, 'pix', axis=2, tiled=True)]
  transfers between devices with their start and end apart: 3 -> 3, of which waited for: 3 -> 3; matrix products, arithmetic and copies ran while one was open for 25% -> 21% of each run, Pallas kernels for 0% -> 0%
where the time goes in v5:
time: 202 us
  waiting for transfers between devices  79.3 us (39%)
  blocking collectives  40.8 us (20%)
  matrix products  28 us (14%)
  local copies, waits for them, and re-layouts  23.8 us (12%)
  between operations  13.6 us (7%)
  starting transfers between devices  10.7 us (5%)
  other arithmetic  5.54 us (3%)
    all_gather x1, waiting for transfers between devices, on_device(): column_piece = lax.all_gather(propagator, 'pix', axis=2, tiled=True)  50.4 us
    all_to_all x1, blocking collectives, on_device(): arrived = lax.all_to_all(depth_bf, ('wave', 'pix'), 0, 0, tiled=True)  40.8 us
    all_to_all x1, waiting for transfers between devices, on_device(): pieces = lax.all_to_all(pieces, 'wave', 0, 0, tiled=True)  27.2 us
    dot_general x1, matrix products, on_device(): jnp.einsum('crzp,pq->crzq', left, stacked, preferred_element_type=jnp.flo...  14.9 us
    dot_general x8, matrix products, dot(): return jnp.einsum(spec, a, b, precision=MATMUL_PRECISION)  13.1 us
    convert_element_type x2, local copies, waits for them, and re-layouts, on_device(): imag_part = spectra[1].astype(jnp.float32)  6.86 us
    all_to_all x1, starting transfers between devices, on_device(): tables = lax.all_to_all(tables, 'wave', 0, 0, tiled=True)  6.37 us
    all_to_all x1, starting transfers between devices, on_device(): pieces = lax.all_to_all(pieces, 'wave', 0, 0, tiled=True)  4.28 us
  transfers between devices with their start and end apart: 3, of which 3 were waited for; matrix products, arithmetic and copies ran while one was open for 21% of the time, Pallas kernels for 0%

profile of v5, /device:TPU:1, one launch (start us, length us, event | category | flops | bytes accessed | tf_op | source)
XLA Modules:
  0.0 201.7 jit_solution(2266722187903991714)
XLA Ops:
  8.7 6.4 %all-to-all-start.1 = ((f32[8,2,2048]{2,1,0:T(2,128)}), f32[8,2,2048]{2,1,0:T(2,128)S(1)}, u32[]{:S(2)}, u32[]{:S(2)}) async-start(f32[8,2,2048]{2,1,0:T(2,128)} %broadcast_in_dim.2), calls=%async_computation.1 | async-start | bytes 262144 | tf_op jit(solution)/shard_map/all_to_all | solution.py:42
  15.0 2.9 %copy.40 = bf16[2,2,2048,128]{2,3,1,0:T(8,128)(2,1)S(1)} copy(bf16[2,2,2048,128]{3,2,1,0:T(8,128)(2,1)} %param.4) | data formatting | bytes 4194304 | tf_op args[0]
  18.0 1.5 copy.41
  20.3 4.3 %all-to-all-start = ((bf16[8,2,2,16,2048]{4,3,2,1,0:T(8,128)(2,1)}), bf16[8,2,2,16,2048]{4,3,2,1,0:T(8,128)(2,1)S(1)}, u32[]{:S(2)}, u32[]{:S(2)}) async-start(bf16[8,2,2,16,2048]{4,3,2,1,0:T(8,128)(2,1)} %copy.41), calls=%async_computation | async-start | bytes 4194304 | tf_op jit(solution)/shard_map/all_to_all | solution.py:38
  25.3 1.9 fusion.101
  27.3 27.2 %all-to-all-done = bf16[8,2,2,16,2048]{4,3,2,1,0:T(8,128)(2,1)S(1)} async-done(((bf16[8,2,2,16,2048]{4,3,2,1,0:T(8,128)(2,1)}), bf16[8,2,2,16,2048]{4,3,2,1,0:T(8,128)(2,1)S(1)}, u32[]{:S(2)}, u32[]{:S(2)}) %all-to-all-start) | async-done | bytes 2097184 | tf_op jit(solution)/shard_map/all_to_all | solution.py:38
  54.5 1.7 slice_convert_fusion.1
  56.2 2.5 %copy.42 = f32[1,2,16,8,2048]{4,3,2,1,0:T(8,128)} copy(f32[1,2,16,8,2048]{4,2,1,0,3:T(8,128)S(1)} %get-tuple-element.7) | data formatting | bytes 4194304 | tf_op jit(solution)/shard_map/convert_element_type | solution.py:47
  58.7 1.7 reshape.94
  60.4 4.1 %copy.43 = f32[1,2,16,8,2048]{4,3,2,1,0:T(8,128)} copy(f32[1,2,16,8,2048]{4,2,1,0,3:T(8,128)} %get-tuple-element.8) | data formatting | bytes 4194304 | tf_op jit(solution)/shard_map/convert_element_type | solution.py:48
  64.6 2.7 %reshape.95 = f32[2,16,128,128]{3,2,1,0:T(8,128)} reshape(f32[1,2,16,8,2048]{4,3,2,1,0:T(8,128)} %copy.43) | data formatting | bytes 4194304 | tf_op jit(solution)/shard_map/convert_element_type | solution.py:48
  67.3 3.1 %fusion.23 = f32[128,2,16,128]{3,0,2,1:T(8,128)S(1)} fusion(f32[2,16,128,128]{3,2,1,0:T(8,128)} %reshape.95, f32[2,16,128,128]{3,2,1,0:T(8,128)S(1)} %reshape.94, f32[128,128]{1,0:T(8,128)S(1)} %bitcast.87, f32[128,128]{1,0:T(8,128)S(1)} %bitcast.91, f32[128,128]{1,0:T(8,128)S(1)} %bitcast.83), kind=kOutput, calls=%fused_computation.28 | convolution fusion | flops 404979712 | bytes 6488064 | tf_op jit(solution)/shard_map/rsak,az->rszk/dot_general | solution.py:19
  70.5 1.4 fusion.22
  71.9 1.4 convolution_subtract_fusion
  73.3 1.4 convolution_add_fusion
  74.8 1.3 fusion.6
  76.1 1.5 fusion.16
  79.0 1.5 fusion.19
  80.7 1.6 copy.46
  82.2 40.8 %all_to_all.15 = bf16[128,2,2,16,128]{4,3,2,1,0:T(8,128)(2,1)S(1)} all-to-all(bf16[128,2,2,16,128]{4,3,2,1,0:T(8,128)(2,1)S(1)} %copy.46), channel_id=1, replica_groups=mesh['wave'=8,'pix'=16] {'wave','pix'}, dimensions={0} | all-to-all | bytes 4194304 | tf_op jit(solution)/shard_map/all_to_all | solution.py:73
  125.8 1.5 copy.50
  127.3 2.2 %maximum_bitcast_fusion = (bf16[1,2,128,4096]{3,2,1,0:T(8,128)(2,1)}, bf16[1,2,128,4096]{3,2,1,0:T(8,128)(2,1)}) fusion(bf16[2,128,2048]{2,1,0:T(8,128)(2,1)S(1)} %neg.3, bf16[2,128,2048]{2,1,0:T(8,128)(2,1)S(1)} %copy.50, bf16[2,128,2048]{2,1,0:T(8,128)(2,1)S(1)} %copy.49), kind=kLoop, calls=%fused_computation.5 | loop fusion | flops 8388608 | bytes 7340032 | tf_op jit(solution)/shard_map/stack | solution.py:81
  129.5 50.4 %all-gather.2.cloned.1.call-done = bf16[2,2048,2048]{2,1,0:T(8,128)(2,1)} async-done(((bf16[2,2048,128]{2,1,0:T(8,128)(2,1)}), bf16[2,2048,2048]{2,1,0:T(8,128)(2,1)}) %all-gather.2.cloned.1.call-update) | async-done | bytes 16777232 | tf_op jit(solution)/shard_map/all_gather | solution.py:78
  180.0 14.9 %fusion = f32[2,2,128,2048]{3,2,1,0:T(8,128)} fusion(bf16[4096,2048,1,1]{1,0,3,2:T(8,128)(2,1)} %bitcast.97, bf16[1,2,128,4096]{3,2,1,0:T(8,128)(2,1)} %get-tuple-element.10, bf16[1,2,128,4096]{3,2,1,0:T(8,128)(2,1)} %get-tuple-element.9), kind=kOutput, calls=%fused_computation | convolution fusion | flops 8592031744 | bytes 25165824 | tf_op jit(solution)/shard_map/crzp,pq->crzq/dot_general | solution.py:88
  (18 shorter events, 7.9 us)
Async XLA Ops:
  6.5 173.4 %all-gather.2.cloned.1.call-start = ((), (), s32[]{:S(2)}) async-start(), calls=%async_computation.3 | async-start | bytes 17825792 | tf_op jit(solution)/shard_map/all_gather | solution.py:78
  8.7 11.6 %all-to-all-start.1 = ((f32[8,2,2048]{2,1,0:T(2,128)}), f32[8,2,2048]{2,1,0:T(2,128)S(1)}, u32[]{:S(2)}, u32[]{:S(2)}) async-start(f32[8,2,2048]{2,1,0:T(2,128)} %broadcast_in_dim.2), calls=%async_computation.1 | async-start | bytes 262144 | tf_op jit(solution)/shard_map/all_to_all | solution.py:42
  20.3 34.2 %all-to-all-start = ((bf16[8,2,2,16,2048]{4,3,2,1,0:T(8,128)(2,1)}), bf16[8,2,2,16,2048]{4,3,2,1,0:T(8,128)(2,1)S(1)}, u32[]{:S(2)}, u32[]{:S(2)}) async-start(bf16[8,2,2,16,2048]{4,3,2,1,0:T(8,128)(2,1)} %copy.41), calls=%async_computation | async-start | bytes 4194304 | tf_op jit(solution)/shard_map/all_to_all | solution.py:38
  67.3 3.2 %copy-start = (f32[2,16,128,128]{3,2,1,0:T(8,128)S(1)}, f32[2,16,128,128]{3,2,1,0:T(8,128)}, u32[]{:S(2)}) copy-start(f32[2,16,128,128]{3,2,1,0:T(8,128)} %reshape.95) | copy-start | bytes 6291460
Sparse Core Ops, SparseCore 0:
  9.6 170.2 all-gather.1

commit v6 on v5

--- a/solution.py
+++ b/solution.py
@@ -3,6 +3,8 @@
 import jax
 import jax.numpy as jnp
 from jax import lax
+from jax.experimental import pallas as pl
+from jax.experimental.pallas import tpu as pltpu
 from jax.sharding import PartitionSpec as P
 
 MATMUL_PRECISION = lax.Precision.HIGH
@@ -85,7 +87,32 @@
         )
     )
     stacked = column_piece.reshape(2 * column_piece.shape[1], column_piece.shape[2])
-    return jnp.einsum("crzp,pq->crzq", left, stacked, preferred_element_type=jnp.float32)
+    image = image_product(left.reshape(-1, stacked.shape[0]), stacked)
+    return image.reshape(left.shape[:-1] + (stacked.shape[1],))
+
+
+def image_kernel(left_ref, right_ref, out_ref):
+    out_ref[...] = jnp.dot(left_ref[...], right_ref[...], preferred_element_type=jnp.float32)
+
+
+def image_product(left, right, tile=256):
+    rows, depth = left.shape
+    columns = right.shape[1]
+    return pl.pallas_call(
+        image_kernel,
+        out_shape=jax.ShapeDtypeStruct((rows, columns), jnp.float32),
+        grid=(columns // tile,),
+        in_specs=[
+            pl.BlockSpec((rows, depth), lambda j: (0, 0)),
+            pl.BlockSpec((depth, tile), lambda j: (0, j)),
+        ],
+        out_specs=pl.BlockSpec((rows, tile), lambda j: (0, j)),
+        cost_estimate=pl.CostEstimate(
+            flops=2 * rows * depth * columns,
+            transcendentals=0,
+            bytes_accessed=2 * rows * depth + 2 * depth * columns + 4 * rows * columns,
+        ),
+    )(left, right)
 
 
 def solution(mesh):

time: 202 us -> 203 us (level)
  Pallas kernels: 0 us -> 15.6 us
  matrix products: 28 us -> 13.1 us
  waiting for transfers between devices: 79.3 us -> 75.3 us
  local copies, waits for them, and re-layouts: 23.8 us -> 27.4 us
    pallas_call x0 -> x1, Pallas kernels: none -> 15.6 us  [image_product(): pl.pallas_call(image_kernel, out_shape=jax.ShapeDtypeStruct((rows, column...]
    dot_general x1 -> x0, matrix products: 14.9 us -> none  [on_device(): jnp.einsum('crzp,pq->crzq', left, stacked, preferred_element_type=jnp.flo...]
    another operation x0 -> x1, local copies, waits for them, and re-layouts: none -> 6.4 us  [on_device(): jnp.stack((jnp.concatenate((depth_real, -depth_imag), axis=-1), jnp.conca...]
    all_gather x1, waiting for transfers between devices: 50.4 us -> 46.5 us  [on_device(): column_piece = lax.all_gather(propagator, 'pix', axis=2, tiled=True)]
  transfers between devices with their start and end apart: 3 -> 3, of which waited for: 3 -> 3; matrix products, arithmetic and copies ran while one was open for 21% -> 23% of each run, Pallas kernels for 0% -> 0%
where the time goes in v6:
time: 203 us; the launch traced here: 202 us
  waiting for transfers between devices  75.3 us (37%)
  blocking collectives  40.8 us (20%)
  local copies, waits for them, and re-layouts  27.4 us (13%)
  Pallas kernels  15.6 us (8%)
  between operations  13.6 us (7%)
  matrix products  13.1 us (6%)
  starting transfers between devices  10.7 us (5%)
  other arithmetic  5.96 us (3%)
    all_gather x1, waiting for transfers between devices, on_device(): column_piece = lax.all_gather(propagator, 'pix', axis=2, tiled=True)  46.5 us
    all_to_all x1, blocking collectives, on_device(): arrived = lax.all_to_all(depth_bf, ('wave', 'pix'), 0, 0, tiled=True)  40.8 us
    all_to_all x1, waiting for transfers between devices, on_device(): pieces = lax.all_to_all(pieces, 'wave', 0, 0, tiled=True)  27.2 us
    pallas_call x1, Pallas kernels, image_product(): pl.pallas_call(image_kernel, out_shape=jax.ShapeDtypeStruct((rows, column...  15.6 us
    dot_general x8, matrix products, dot(): return jnp.einsum(spec, a, b, precision=MATMUL_PRECISION)  13.1 us
    convert_element_type x2, local copies, waits for them, and re-layouts, on_device(): imag_part = spectra[1].astype(jnp.float32)  6.86 us
    another operation x1, local copies, waits for them, and re-layouts, on_device(): jnp.stack((jnp.concatenate((depth_real, -depth_imag), axis=-1), jnp.conca...  6.4 us
    all_to_all x1, starting transfers between devices, on_device(): tables = lax.all_to_all(tables, 'wave', 0, 0, tiled=True)  6.37 us
  transfers between devices with their start and end apart: 3, of which 3 were waited for; matrix products, arithmetic and copies ran while one was open for 23% of the time, Pallas kernels for 0%

profile of v6, /device:TPU:1, one launch (start us, length us, event | category | flops | bytes accessed | tf_op | source)
XLA Modules:
  0.0 202.4 jit_solution(8178506824166382873)
XLA Ops:
  8.7 6.4 %all-to-all-start.1 = ((f32[8,2,2048]{2,1,0:T(2,128)}), f32[8,2,2048]{2,1,0:T(2,128)S(1)}, u32[]{:S(2)}, u32[]{:S(2)}) async-start(f32[8,2,2048]{2,1,0:T(2,128)} %broadcast_in_dim.2), calls=%async_computation.1 | async-start | bytes 262144 | tf_op jit(solution)/shard_map/all_to_all | solution.py:44
  15.0 2.9 %copy.31 = bf16[2,2,2048,128]{2,3,1,0:T(8,128)(2,1)S(1)} copy(bf16[2,2,2048,128]{3,2,1,0:T(8,128)(2,1)} %param.4) | data formatting | bytes 4194304 | tf_op args[0]
  18.0 1.5 copy.32
  20.3 4.3 %all-to-all-start = ((bf16[8,2,2,16,2048]{4,3,2,1,0:T(8,128)(2,1)}), bf16[8,2,2,16,2048]{4,3,2,1,0:T(8,128)(2,1)S(1)}, u32[]{:S(2)}, u32[]{:S(2)}) async-start(bf16[8,2,2,16,2048]{4,3,2,1,0:T(8,128)(2,1)} %copy.32), calls=%async_computation | async-start | bytes 4194304 | tf_op jit(solution)/shard_map/all_to_all | solution.py:40
  25.3 1.9 fusion.96
  27.3 27.2 %all-to-all-done = bf16[8,2,2,16,2048]{4,3,2,1,0:T(8,128)(2,1)S(1)} async-done(((bf16[8,2,2,16,2048]{4,3,2,1,0:T(8,128)(2,1)}), bf16[8,2,2,16,2048]{4,3,2,1,0:T(8,128)(2,1)S(1)}, u32[]{:S(2)}, u32[]{:S(2)}) %all-to-all-start) | async-done | bytes 2097184 | tf_op jit(solution)/shard_map/all_to_all | solution.py:40
  54.5 1.7 slice_convert_fusion.1
  56.2 2.5 %copy.33 = f32[1,2,16,8,2048]{4,3,2,1,0:T(8,128)} copy(f32[1,2,16,8,2048]{4,2,1,0,3:T(8,128)S(1)} %get-tuple-element.7) | data formatting | bytes 4194304 | tf_op jit(solution)/shard_map/convert_element_type | solution.py:49
  58.7 1.7 reshape.102
  60.4 4.1 %copy.34 = f32[1,2,16,8,2048]{4,3,2,1,0:T(8,128)} copy(f32[1,2,16,8,2048]{4,2,1,0,3:T(8,128)} %get-tuple-element.8) | data formatting | bytes 4194304 | tf_op jit(solution)/shard_map/convert_element_type | solution.py:50
  64.6 2.7 %reshape.103 = f32[2,16,128,128]{3,2,1,0:T(8,128)} reshape(f32[1,2,16,8,2048]{4,3,2,1,0:T(8,128)} %copy.34) | data formatting | bytes 4194304 | tf_op jit(solution)/shard_map/convert_element_type | solution.py:50
  67.3 3.1 %fusion.19 = f32[128,2,16,128]{3,0,2,1:T(8,128)S(1)} fusion(f32[2,16,128,128]{3,2,1,0:T(8,128)} %reshape.103, f32[2,16,128,128]{3,2,1,0:T(8,128)S(1)} %reshape.102, f32[128,128]{1,0:T(8,128)S(1)} %bitcast.86, f32[128,128]{1,0:T(8,128)S(1)} %bitcast.90, f32[128,128]{1,0:T(8,128)S(1)} %bitcast.82), kind=kOutput, calls=%fused_computation.25 | convolution fusion | flops 404979712 | bytes 6488064 | tf_op jit(solution)/shard_map/rsak,az->rszk/dot_general | solution.py:21
  70.5 1.4 fusion.18
  71.9 1.4 convolution_subtract_fusion
  73.3 1.4 convolution_add_fusion
  74.8 1.3 fusion.2
  76.1 1.5 fusion.12
  79.0 1.5 fusion.15
  80.7 1.6 copy.37
  82.2 40.8 %all_to_all.15 = bf16[128,2,2,16,128]{4,3,2,1,0:T(8,128)(2,1)S(1)} all-to-all(bf16[128,2,2,16,128]{4,3,2,1,0:T(8,128)(2,1)S(1)} %copy.37), channel_id=1, replica_groups=mesh['wave'=8,'pix'=16] {'wave','pix'}, dimensions={0} | all-to-all | bytes 4194304 | tf_op jit(solution)/shard_map/all_to_all | solution.py:75
  124.7 2.4 %pad_maximum_fusion = bf16[2,2,128,4096]{2,3,1,0:T(8,128)(2,1)} fusion(bf16[1,2,128,4096]{2,3,1,0:T(8,128)(2,1)S(1)} %get-tuple-element.10, bf16[1,2,128,4096]{2,3,1,0:T(8,128)(2,1)S(1)} %get-tuple-element.9), kind=kLoop, calls=%fused_computation | loop fusion | flops 2097152 | bytes 8388608 | tf_op jit(solution)/shard_map/stack | solution.py:83
  127.1 6.4 %copy.40 = bf16[2,2,128,4096]{3,2,1,0:T(8,128)(2,1)} copy(bf16[2,2,128,4096]{2,3,1,0:T(8,128)(2,1)} %pad_maximum_fusion) | data formatting | bytes 8388608 | tf_op jit(solution)/shard_map/stack | solution.py:83
  133.5 46.5 %all-gather.2.cloned.1.call-done = bf16[2,2048,2048]{2,1,0:T(8,128)(2,1)} async-done(((bf16[2,2048,128]{2,1,0:T(8,128)(2,1)}), bf16[2,2048,2048]{2,1,0:T(8,128)(2,1)}) %all-gather.2.cloned.1.call-update) | async-done | bytes 16777232 | tf_op jit(solution)/shard_map/all_gather | solution.py:80
  180.0 15.6 %shard_map.46 = f32[512,2048]{1,0:T(8,128)} custom-call(bf16[512,4096]{1,0:T(8,128)(2,1)} %bitcast.81, bf16[4096,2048]{1,0:T(8,128)(2,1)} %bitcast.96), custom_call_target="tpu_custom_call" | custom-call | flops 8589934592 | bytes 25165824 | tf_op jit(solution)/shard_map/pallas_call | solution.py:101
  (18 shorter events, 6.8 us)
Async XLA Ops:
  6.5 173.4 %all-gather.2.cloned.1.call-start = ((), (), s32[]{:S(2)}) async-start(), calls=%async_computation.3 | async-start | bytes 17825792 | tf_op jit(solution)/shard_map/all_gather | solution.py:80
  8.7 11.6 %all-to-all-start.1 = ((f32[8,2,2048]{2,1,0:T(2,128)}), f32[8,2,2048]{2,1,0:T(2,128)S(1)}, u32[]{:S(2)}, u32[]{:S(2)}) async-start(f32[8,2,2048]{2,1,0:T(2,128)} %broadcast_in_dim.2), calls=%async_computation.1 | async-start | bytes 262144 | tf_op jit(solution)/shard_map/all_to_all | solution.py:44
  20.3 34.2 %all-to-all-start = ((bf16[8,2,2,16,2048]{4,3,2,1,0:T(8,128)(2,1)}), bf16[8,2,2,16,2048]{4,3,2,1,0:T(8,128)(2,1)S(1)}, u32[]{:S(2)}, u32[]{:S(2)}) async-start(bf16[8,2,2,16,2048]{4,3,2,1,0:T(8,128)(2,1)} %copy.32), calls=%async_computation | async-start | bytes 4194304 | tf_op jit(solution)/shard_map/all_to_all | solution.py:40
  67.3 3.2 %copy-start = (f32[2,16,128,128]{3,2,1,0:T(8,128)S(1)}, f32[2,16,128,128]{3,2,1,0:T(8,128)}, u32[]{:S(2)}) copy-start(f32[2,16,128,128]{3,2,1,0:T(8,128)} %reshape.103) | copy-start | bytes 6291460
Sparse Core Ops, SparseCore 0:
  9.6 170.2 all-gather.1

commit v7 on v4

--- a/solution.py
+++ b/solution.py
@@ -6,6 +6,8 @@
 from jax.sharding import PartitionSpec as P
 
 HIGHEST_PRECISION = lax.Precision.HIGHEST
+PIX = ("chip", "core")
+ALL = ("wave",) + PIX
 
 
 def twiddle_table(left_index, right_index, modulus, scale=1.0):
@@ -26,7 +28,7 @@
     wave_span = raw_spectra.shape[2]
     pix_local = raw_spectra.shape[3]
     wave_count = lax.axis_size("wave")
-    pix_count = lax.axis_size("pix")
+    pix_count = lax.axis_size(PIX)
     devices = wave_count * pix_count
     length = wave_span * wave_count
     sub_pix = pix_local // wave_count
@@ -70,27 +72,38 @@
         "rszk,kt->trsz", mixed_real, mixed_imag, big_cos, big_sin
     )
     depth_bf = jnp.stack((out_real, out_imag), axis=1).astype(jnp.bfloat16)
-    arrived = lax.all_to_all(depth_bf, ("wave", "pix"), 0, 0, tiled=True)
+    arrived = lax.all_to_all(depth_bf, ALL, 0, 0, tiled=True)
     arrived = arrived.reshape(wave_count, pix_count, 2, row_count, sub_pix, first)
     depth_field = jnp.transpose(arrived, (2, 3, 5, 1, 0, 4)).reshape(
         2, row_count, first, pix_count * pix_local
     )
-    column_piece = lax.all_gather(propagator, "pix", axis=2, tiled=True)
-    depth_real = depth_field[0]
-    depth_imag = depth_field[1]
+    same_core = lax.all_gather(propagator, "chip", axis=0)
+    pairs = [(index, index ^ 1) for index in range(wave_count * pix_count)]
+    sibling_depth = lax.ppermute(depth_field, ALL, pairs)
+    blocks = jnp.stack((depth_field, sibling_depth), axis=2)
     left = jnp.stack(
         (
-            jnp.concatenate((depth_real, -depth_imag), axis=-1),
-            jnp.concatenate((depth_imag, depth_real), axis=-1),
+            jnp.stack((blocks[0], -blocks[1]), axis=-2),
+            jnp.stack((blocks[1], blocks[0]), axis=-2),
         )
     )
-    stacked = column_piece.reshape(2 * column_piece.shape[1], column_piece.shape[2])
-    return jnp.einsum("crzp,pq->crzq", left, stacked, preferred_element_type=jnp.float32)
+    product = jnp.einsum(
+        "drbzcp,kcpj->drbzkj", left, same_core, preferred_element_type=jnp.float32
+    )
+    received = lax.ppermute(product[:, :, 1], ALL, pairs)
+    mine = product[:, :, 0]
+    own_first = lax.axis_index("core") == 0
+    image = jnp.where(
+        own_first, jnp.stack((mine, received), axis=4), jnp.stack((received, mine), axis=4)
+    )
+    return image.reshape(2, row_count, first, pix_count * pix_local)
 
 
 def solution(mesh):
-    in_specs = (P(None, None, "wave", "pix"), P("wave"), P("wave"), P(None, None, "pix"))
-    out_specs = P(None, None, ("wave", "pix"), None)
+    wave_count, pix_count = mesh.devices.shape
+    split_mesh = jax.sharding.Mesh(mesh.devices.reshape(wave_count, pix_count // 2, 2), ALL)
+    in_specs = (P(None, None, "wave", PIX), P("wave"), P("wave"), P(None, None, PIX))
+    out_specs = P(None, None, ALL, None)
     return jax.shard_map(
-        on_device, mesh=mesh, in_specs=in_specs, out_specs=out_specs, check_vma=False
+        on_device, mesh=split_mesh, in_specs=in_specs, out_specs=out_specs, check_vma=False
     )

time: 202 us -> 205 us (1.015)
  waiting for transfers between devices: 72.1 us -> 53 us
  local copies, waits for them, and re-layouts: 23.6 us -> 35.2 us
  other arithmetic: 5.54 us -> 12.5 us
  blocking collectives: 40.8 us -> 43.7 us
  matrix products: 35.4 us -> 33.1 us
  starting transfers between devices: 10.7 us -> 12.9 us
    all_gather x1, waiting for transfers between devices: 43.2 us -> 18.9 us  [on_device(): same_core = lax.all_gather(propagator, 'chip', axis=0)]
    select_n x0 -> x2, local copies, waits for them, and re-layouts: none -> 7.57 us  [on_device(): jnp.where(own_first, jnp.stack((mine, received), axis=4), jnp.stack((rece...]
    ppermute x0 -> x2, waiting for transfers between devices: none -> 5.31 us  [the longest x1 4.13 us: on_device(): received = lax.ppermute(product[:, :, 1], ALL, pairs)]
    another operation x0 -> x2, local copies, waits for them, and re-layouts: none -> 4.65 us  [the longest x1 2.94 us: on_device(): blocks = jnp.stack((depth_field, sibling_depth), axis=2)]
    another operation x1 -> x2, other arithmetic: 2.22 us -> 5.14 us  [the longest x1 3.72 us: on_device(): jnp.stack((jnp.stack((blocks[0], -blocks[1]), axis=-2), jnp.stack((blocks...]
    all_to_all x1, blocking collectives: 40.8 us -> 43.7 us  [on_device(): arrived = lax.all_to_all(depth_bf, ALL, 0, 0, tiled=True)]
    select_n x0 -> x1, other arithmetic: none -> 2.75 us  [on_device(): jnp.where(own_first, jnp.stack((mine, received), axis=4), jnp.stack((rece...]
    reshape x0 -> x1, local copies, waits for them, and re-layouts: none -> 2.63 us  [on_device(): jnp.transpose(arrived, (2, 3, 5, 1, 0, 4))]
  transfers between devices with their start and end apart: 3 -> 5, of which waited for: 3 -> 5; matrix products, arithmetic and copies ran while one was open for 25% -> 28% of each run, Pallas kernels for 0% -> 0%
where the time goes in v7:
time: 205 us; the launch traced here: 204 us
  waiting for transfers between devices  53 us (26%)
  blocking collectives  43.7 us (21%)
  local copies, waits for them, and re-layouts  35.2 us (17%)
  matrix products  33.1 us (16%)
  between operations  13.6 us (7%)
  starting transfers between devices  12.9 us (6%)
  other arithmetic  12.5 us (6%)
    all_to_all x1, blocking collectives, on_device(): arrived = lax.all_to_all(depth_bf, ALL, 0, 0, tiled=True)  43.7 us
    all_to_all x1, waiting for transfers between devices, on_device(): pieces = lax.all_to_all(pieces, 'wave', 0, 0, tiled=True)  27.2 us
    dot_general x8, matrix products, dot(): return jnp.einsum(spec, a, b, precision=HIGHEST_PRECISION)  20.5 us
    all_gather x1, waiting for transfers between devices, on_device(): same_core = lax.all_gather(propagator, 'chip', axis=0)  18.9 us
    dot_general x1, matrix products, on_device(): jnp.einsum('drbzcp,kcpj->drbzkj', left, same_core, preferred_element_type...  12.6 us
    select_n x2, local copies, waits for them, and re-layouts, on_device(): jnp.where(own_first, jnp.stack((mine, received), axis=4), jnp.stack((rece...  7.57 us
    convert_element_type x2, local copies, waits for them, and re-layouts, on_device(): imag_part = spectra[1].astype(jnp.float32)  6.88 us
    all_to_all x1, starting transfers between devices, on_device(): tables = lax.all_to_all(tables, 'wave', 0, 0, tiled=True)  6.37 us
  transfers between devices with their start and end apart: 5, of which 5 were waited for; matrix products, arithmetic and copies ran while one was open for 28% of the time, Pallas kernels for 0%

profile of v7, /device:TPU:1, one launch (start us, length us, event | category | flops | bytes accessed | tf_op | source)
XLA Modules:
  0.0 204.0 jit_solution(2292108386884907753)
XLA Ops:
  8.7 6.4 %all-to-all-start.1 = ((f32[8,2,2048]{2,1,0:T(2,128)}), f32[8,2,2048]{2,1,0:T(2,128)S(1)}, u32[]{:S(2)}, u32[]{:S(2)}) async-start(f32[8,2,2048]{2,1,0:T(2,128)} %broadcast_in_dim.2), calls=%async_computation.1 | async-start | bytes 262144 | tf_op jit(solution)/shard_map/all_to_all | solution.py:44
  15.0 2.9 %copy.48 = bf16[2,2,2048,128]{2,3,1,0:T(8,128)(2,1)S(1)} copy(bf16[2,2,2048,128]{3,2,1,0:T(8,128)(2,1)} %param.4) | data formatting | bytes 4194304 | tf_op args[0]
  20.3 4.3 %all-to-all-start = ((bf16[8,2,2,16,2048]{4,3,2,1,0:T(8,128)(2,1)}), bf16[8,2,2,16,2048]{4,3,2,1,0:T(8,128)(2,1)S(1)}, u32[]{:S(2)}, u32[]{:S(2)}) async-start(bf16[8,2,2,16,2048]{4,3,2,1,0:T(8,128)(2,1)} %copy.49), calls=%async_computation | async-start | bytes 4194304 | tf_op jit(solution)/shard_map/all_to_all | solution.py:40
  27.3 27.2 %all-to-all-done = bf16[8,2,2,16,2048]{4,3,2,1,0:T(8,128)(2,1)S(1)} async-done(((bf16[8,2,2,16,2048]{4,3,2,1,0:T(8,128)(2,1)}), bf16[8,2,2,16,2048]{4,3,2,1,0:T(8,128)(2,1)S(1)}, u32[]{:S(2)}, u32[]{:S(2)}) %all-to-all-start) | async-done | bytes 2097184 | tf_op jit(solution)/shard_map/all_to_all | solution.py:40
  56.2 2.6 %copy.50 = f32[1,2,16,8,2048]{4,3,2,1,0:T(8,128)} copy(f32[1,2,16,8,2048]{4,2,1,0,3:T(8,128)S(1)} %get-tuple-element.11) | data formatting | bytes 4194304 | tf_op jit(solution)/shard_map/convert_element_type | solution.py:49
  60.5 4.2 %copy.51 = f32[1,2,16,8,2048]{4,3,2,1,0:T(8,128)} copy(f32[1,2,16,8,2048]{4,2,1,0,3:T(8,128)} %get-tuple-element.12) | data formatting | bytes 4194304 | tf_op jit(solution)/shard_map/convert_element_type | solution.py:50
  64.7 2.7 %reshape.105 = f32[2,16,128,128]{3,2,1,0:T(8,128)} reshape(f32[1,2,16,8,2048]{4,3,2,1,0:T(8,128)} %copy.51) | data formatting | bytes 4194304 | tf_op jit(solution)/shard_map/convert_element_type | solution.py:50
  67.4 4.1 %fusion.26 = f32[128,2,16,128]{3,0,2,1:T(8,128)S(1)} fusion(f32[2,16,128,128]{3,2,1,0:T(8,128)} %reshape.105, f32[2,16,128,128]{3,2,1,0:T(8,128)S(1)} %reshape.104, f32[128,128]{1,0:T(8,128)S(1)} %bitcast.113, f32[128,128]{1,0:T(8,128)S(1)} %bitcast.117, f32[128,128]{1,0:T(8,128)S(1)} %bitcast.109), kind=kOutput, calls=%fused_computation.38 | convolution fusion | flops 807632896 | bytes 6488064 | tf_op jit(solution)/shard_map/rsak,az->rszk/dot_general | solution.py:21
  71.4 2.3 %fusion.25 = f32[128,2,16,128]{3,0,2,1:T(8,128)S(1)} fusion(f32[2,16,128,128]{3,2,1,0:T(8,128)S(1)} %copy-done, f32[2,16,128,128]{3,2,1,0:T(8,128)S(1)} %reshape.104, f32[128,128]{1,0:T(8,128)S(1)} %bitcast.114, f32[128,128]{1,0:T(8,128)S(1)} %bitcast.118, f32[128,128]{1,0:T(8,128)S(1)} %bitcast.110), kind=kOutput, calls=%fused_computation.37 | convolution fusion | flops 807632896 | bytes 6488064 | tf_op jit(solution)/shard_map/rsak,az->rszk/dot_general | solution.py:21
  73.8 2.3 %convolution_subtract_fusion = f32[128,2,16,128]{3,0,2,1:T(8,128)S(1)} fusion(f32[128,2,16,128]{3,0,2,1:T(8,128)S(1)} %fusion.26, f32[2,16,128,128]{3,2,1,0:T(8,128)S(1)} %copy-done, f32[2,16,128,128]{3,2,1,0:T(8,128)S(1)} %reshape.104, f32[128,128]{1,0:T(8,128)S(1)} %bitcast.115, f32[128,128]{1,0:T(8,128)S(1)} %bitcast.119, f32[128,128]{1,0:T(8,128)S(1)} %bitcast.111), kind=kOutput, calls=%fused_computation.32 | convolution fusion | flops 808157184 | bytes 8585216 | tf_op jit(solution)/shard_map/rsak,az->rszk/dot_general | solution.py:21
  76.1 2.4 %convolution_add_fusion = f32[128,2,16,128]{3,0,2,1:T(8,128)S(1)} fusion(f32[128,2,16,128]{3,0,2,1:T(8,128)S(1)} %fusion.25, f32[2,16,128,128]{3,2,1,0:T(8,128)S(1)} %copy-done, f32[2,16,128,128]{3,2,1,0:T(8,128)S(1)} %reshape.104, f32[128,128]{1,0:T(8,128)S(1)} %bitcast.116, f32[128,128]{1,0:T(8,128)S(1)} %bitcast.120, f32[128,128]{1,0:T(8,128)S(1)} %bitcast.112), kind=kOutput, calls=%fused_computation.31 | convolution fusion | flops 808157184 | bytes 8585216 | tf_op jit(solution)/shard_map/rsak,az->rszk/dot_general | solution.py:21
  78.5 2.2 %fusion.9 = f32[128,2,16,128]{3,0,2,1:T(8,128)S(1)} fusion(f32[128,2,16,128]{3,0,2,1:T(8,128)S(1)} %convolution_add_fusion, f32[128,2,16,128]{3,0,2,1:T(8,128)S(1)} %convolution_subtract_fusion, f32[128,128]{1,0:T(8,128)S(1)} %copy.53, f32[128,128]{1,0:T(8,128)S(1)} %copy.52), kind=kOutput, calls=%fused_computation.19 | convolution fusion | flops 807124992 | bytes 6422528 | tf_op jit(solution)/shard_map/rszk,kt->trsz/dot_general | solution.py:21
  80.7 2.6 %fusion.19 = bf16[128,1,2,16,128]{4,0,3,2,1:T(8,128)(2,1)S(1)} fusion(f32[128,2,16,128]{3,0,2,1:T(8,128)S(1)} %fusion.9, f32[128,2,16,128]{3,0,2,1:T(8,128)S(1)} %convolution_add_fusion, f32[128,2,16,128]{3,0,2,1:T(8,128)S(1)} %convolution_subtract_fusion, f32[128,128]{1,0:T(8,128)S(1)} %copy.53, f32[128,128]{1,0:T(8,128)S(1)} %copy.52), kind=kOutput, calls=%fused_computation.33 | convolution fusion | flops 808173568 | bytes 7471104 | tf_op jit(solution)/shard_map/rszk,kt->trsz/dot_general | solution.py:21
  83.3 2.2 %fusion.7 = f32[128,2,16,128]{3,0,2,1:T(8,128)S(1)} fusion(f32[128,2,16,128]{3,0,2,1:T(8,128)S(1)} %convolution_add_fusion, f32[128,2,16,128]{3,0,2,1:T(8,128)S(1)} %convolution_subtract_fusion, f32[128,128]{1,0:T(8,128)S(1)} %copy.53, f32[128,128]{1,0:T(8,128)S(1)} %copy.52), kind=kOutput, calls=%fused_computation.17 | convolution fusion | flops 807124992 | bytes 6422528 | tf_op jit(solution)/shard_map/rszk,kt->trsz/dot_general | solution.py:21
  85.6 2.4 %fusion.22 = bf16[128,1,2,16,128]{4,0,3,2,1:T(8,128)(2,1)S(1)} fusion(f32[128,2,16,128]{3,0,2,1:T(8,128)S(1)} %fusion.7, f32[128,2,16,128]{3,0,2,1:T(8,128)S(1)} %convolution_add_fusion, f32[128,2,16,128]{3,0,2,1:T(8,128)S(1)} %convolution_subtract_fusion, f32[128,128]{1,0:T(8,128)S(1)} %copy.53, f32[128,128]{1,0:T(8,128)S(1)} %copy.52), kind=kOutput, calls=%fused_computation.34 | convolution fusion | flops 808173568 | bytes 7471104 | tf_op jit(solution)/shard_map/rszk,kt->trsz/dot_general | solution.py:21
  89.5 43.7 %all_to_all.15 = bf16[128,2,2,16,128]{4,3,2,1,0:T(8,128)(2,1)S(1)} all-to-all(bf16[128,2,2,16,128]{4,3,2,1,0:T(8,128)(2,1)S(1)} %copy.54), channel_id=1, replica_groups=mesh['wave'=8,'chip'=8,'core'=2] {'wave','chip','core'}, dimensions={0} | all-to-all | bytes 4194304 | tf_op jit(solution)/shard_map/all_to_all | solution.py:75
  133.8 2.6 %copy.57 = bf16[2,2,128,2048]{3,2,1,0:T(8,128)(2,1)} copy(bf16[2,2,128,2048]{2,3,1,0:T(8,128)(2,1)S(1)} %bitcast.103) | data formatting | bytes 4194304 | tf_op jit(solution)/shard_map/reshape | solution.py:77
  137.5 2.9 %copy.58 = bf16[2,2,1,128,2048]{4,3,2,1,0:T(8,128)(2,1)S(1)} copy(bf16[2,2,1,128,2048]{3,4,1,0,2:T(8,128)(2,1)} %bitcast.104) | data formatting | bytes 4194304 | tf_op jit(solution)/shard_map/stack;reshape | solution.py:83
  144.6 3.7 %maximum_bitcast_fusion.2 = (bf16[1,2,2,128,2,2048]{5,3,4,2,1,0:T(8,128)(2,1)}, bf16[1,2,2,128,2,2048]{5,3,4,2,1,0:T(8,128)(2,1)}) fusion(bf16[2,2,128,1,2048]{4,2,3,1,0:T(8,128)(2,1)S(1)} %get-tuple-element.5, bf16[2,2,128,1,2048]{4,2,3,1,0:T(8,128)(2,1)S(1)} %fusion.5, bf16[2,2,128,1,2048]{4,2,3,1,0:T(8,128)(2,1)S(1)} %get-tuple-element.6), kind=kLoop, calls=%fused_computation.6 | loop fusion | flops 4194304 | bytes 14680064 | tf_op jit(solution)/shard_map/stack | solution.py:84
  148.3 18.9 %all-gather.3.cloned.1.call-done = bf16[16,2048,128]{2,1,0:T(8,128)(2,1)} async-done(((bf16[2,2048,128]{2,1,0:T(8,128)(2,1)}), bf16[16,2048,128]{2,1,0:T(8,128)(2,1)}) %all-gather.3.cloned.1.call-update) | async-done | bytes 8388624 | tf_op jit(solution)/shard_map/all_gather | solution.py:80
  167.2 12.6 %fusion.3 = f32[2,2,2,128,8,128]{3,5,4,2,1,0:T(8,128)S(1)} fusion(bf16[8,2,2048,128,1,1,1]{3,2,1,0,6,5,4:T(8,128)(2,1)} %bitcast.123, bf16[1,2,2,128,2,2048]{5,3,4,2,1,0:T(8,128)(2,1)} %get-tuple-element.10, bf16[1,2,2,128,2,2048]{5,3,4,2,1,0:T(8,128)(2,1)} %get-tuple-element.9), kind=kOutput, calls=%fused_computation.9 | convolution fusion | flops 8606711808 | bytes 20971520 | tf_op jit(solution)/shard_map/drbzcp,kcpj->drbzkj/dot_general | solution.py:90
  182.7 4.1 %collective-permute-done.1 = f32[2,2,128,8,128]{2,4,3,1,0:T(8,128)} collective-permute-done((f32[2,2,128,8,128]{2,4,3,1,0:T(8,128)}, f32[2,2,128,8,128]{2,4,3,1,0:T(8,128)}, u32[]{:S(2)}, u32[]{:S(2)}) %collective-permute-start.1) | collective-permute-done | bytes 2097184 | tf_op jit(solution)/shard_map/ppermute | solution.py:93
  186.8 2.7 %maximum_select_fusion = f32[2,2,128,8,2,128]{2,5,3,1,0,4:T(8,128)S(1)} fusion(f32[2,2,128,8,1,128]{2,5,3,1,0,4:T(8,128)} %bitcast.43, f32[2,2,128,8,1,128]{2,5,3,1,0,4:T(8,128)S(1)} %get-tuple-element.7, pred[]{:T(512)S(6)} %eq.7), kind=kLoop, calls=%fused_computation.8 | loop fusion | flops 3145728 | bytes 8388609 | tf_op jit(solution)/shard_map/jit(_where)/select_n | solution.py:96
  191.8 5.3 %copy.62 = f32[2,2,128,2048]{3,2,1,0:T(8,128)} copy(f32[2,2,128,2048]{2,3,1,0:T(8,128)} %bitcast.105) | data formatting | bytes 8388608 | tf_op jit(solution)/shard_map/jit(_where)/select_n | solution.py:96
  (27 shorter events, 22.9 us)
Async XLA Ops:
  6.5 160.7 %all-gather.3.cloned.1.call-start = ((), (), s32[]{:S(2)}) async-start(), calls=%async_computation.3 | async-start | bytes 9437184 | tf_op jit(solution)/shard_map/all_gather | solution.py:80
  8.7 11.6 %all-to-all-start.1 = ((f32[8,2,2048]{2,1,0:T(2,128)}), f32[8,2,2048]{2,1,0:T(2,128)S(1)}, u32[]{:S(2)}, u32[]{:S(2)}) async-start(f32[8,2,2048]{2,1,0:T(2,128)} %broadcast_in_dim.2), calls=%async_computation.1 | async-start | bytes 262144 | tf_op jit(solution)/shard_map/all_to_all | solution.py:44
  20.3 34.2 %all-to-all-start = ((bf16[8,2,2,16,2048]{4,3,2,1,0:T(8,128)(2,1)}), bf16[8,2,2,16,2048]{4,3,2,1,0:T(8,128)(2,1)S(1)}, u32[]{:S(2)}, u32[]{:S(2)}) async-start(bf16[8,2,2,16,2048]{4,3,2,1,0:T(8,128)(2,1)} %copy.49), calls=%async_computation | async-start | bytes 4194304 | tf_op jit(solution)/shard_map/all_to_all | solution.py:40
  67.4 4.1 %copy-start = (f32[2,16,128,128]{3,2,1,0:T(8,128)S(1)}, f32[2,16,128,128]{3,2,1,0:T(8,128)}, u32[]{:S(2)}) copy-start(f32[2,16,128,128]{3,2,1,0:T(8,128)} %reshape.105) | copy-start | bytes 6291460
  133.8 2.6 %copy-start.1 = (bf16[2,2,128,16,8,16]{2,5,4,3,1,0:T(8,128)(2,1)}, bf16[2,2,128,16,8,16]{2,5,4,3,1,0:T(8,128)(2,1)S(1)}, u32[]{:S(2)}) copy-start(bf16[2,2,128,16,8,16]{2,5,4,3,1,0:T(8,128)(2,1)S(1)} %copy.55) | copy-start | bytes 6291460
  136.5 5.2 %collective-permute-start = (bf16[2,2,128,2048]{3,2,1,0:T(8,128)(2,1)}, bf16[2,2,128,2048]{3,2,1,0:T(8,128)(2,1)}, u32[]{:S(2)}, u32[]{:S(2)}) collective-permute-start(bf16[2,2,128,2048]{3,2,1,0:T(8,128)(2,1)} %copy.57), channel_id=1, source_target_pairs={{0,1},{1,0},{2,3},{3,2},{4,5},{5,4},{6,7},{7,6},{8,9},{9,8},{10,11... | collective-permute-start | bytes 6291464 | tf_op jit(solution)/shard_map/ppermute | solution.py:82
  181.5 5.3 %collective-permute-start.1 = (f32[2,2,128,8,128]{2,4,3,1,0:T(8,128)}, f32[2,2,128,8,128]{2,4,3,1,0:T(8,128)}, u32[]{:S(2)}, u32[]{:S(2)}) collective-permute-start(f32[2,2,128,8,128]{2,4,3,1,0:T(8,128)} %get-tuple-element.8), channel_id=1, source_target_pairs={{0,1},{1,0},{2,3},{3,2},{4,5},{5,4},{6,7},{7,6},{8,9},{9,8},{10,11... | collective-permute-start | bytes 6291464 | tf_op jit(solution)/shard_map/ppermute | solution.py:93
Sparse Core Ops, SparseCore 0:
  9.7 157.4 all-gather.2
